TPU v7x, 128 devices: a whole 4x4x4 slice. The times are simulated.
128 devices in a mesh: orbits: 4 (over z), rows: 8 (over x, core), cols: 4 (over y).
Axes of the slice: x: 4, y: 4, z: 4, core: 2. Of those that a mesh axis runs over, the one named last changes fastest.
Arguments:
- obs_feat: bfloat16 [524288, 128], P(('orbits', 'rows', 'cols')), may hold values from -6 to 6
- obs_offset: bfloat16 [2, 524288], P(None, ('orbits', 'rows', 'cols')), may hold values from -0.5 to 0.5
- obs_cells: int32 [16, 524288], P(None, ('orbits', 'rows', 'cols')), may hold values from 0 to 255, as said below
- block_tile: int32 [4096], P(('orbits', 'rows', 'cols')), may hold values from 0 to 31, as said below
- block_patch: int32 [4096], P(('orbits', 'rows', 'cols')), may hold values from 0 to 31
- w_embed: bfloat16 [128, 128], replicated, may hold values from -0.5 to 0.5
- b_embed: float32 [128], replicated, may hold values from -3 to 3
- w_proj: bfloat16 [128, 128], replicated, may hold values from -0.5 to 0.5
- b_proj: float32 [128], replicated, may hold values from -3 to 3
- density_weight: float32 [128], replicated, may hold values from -4 to 4
- w_first: bfloat16 [3, 3, 128, 128], replicated, may hold values from -0.1875 to 0.1875
- b_first: float32 [128], replicated, may hold values from -3 to 3
- w_second: bfloat16 [3, 3, 128, 128], replicated, may hold values from -0.1875 to 0.1875
- b_second: float32 [128], replicated, may hold values from -3 to 3
Outputs:
- obs_out: bfloat16 [524288, 128], P(('orbits', 'rows', 'cols'))
- grid_out: bfloat16 [512, 512, 128], P(('orbits', 'rows'), 'cols')
Inputs may be any that keep to these rules, and one draw needn't show every extreme that they name: `obs_cells`: column o is a 4 by 4 window of cells of a 8 by 32 patch: entry k is (a + k // 4) * 32 + b + k % 4 with 0 <= a <= 4 and 0 <= b <= 28. `block_tile`: tile t is the grid block of the devices with rows index t // 4 and cols index t % 4. Of the 32 blocks of one device, at most 2 name one tile, so one tile gets at most 64 blocks from the devices of one orbits index.
All inputs are finite; a program needn't handle non-finite values.
Results may differ from a plain program's by a relative error of at most 0.013.
Values may be sent and summed in bfloat16 or wider, within the bound.
A program may use at most 64 MiB of HBM per device.

v0:
```python
import jax
import jax.numpy as jnp
from jax import lax
from jax.sharding import PartitionSpec as P

KN = 16
PH = 8
PW = 32
SR = 16
TC = 128


inverse_width = 0.5


def extended(x, sides, width):
    for axis, dim in sides:
        size, length = (lax.axis_size(axis), x.shape[dim])
        up = [(i, (i + 1) % size) for i in range(size - 1)]
        down = [(j, i) for i, j in up]
        last = lax.slice_in_dim(x, length - width, length, axis=dim)
        initial = lax.slice_in_dim(x, 0, width, axis=dim)
        before = lax.ppermute(last, axis, up)
        after = lax.ppermute(initial, axis, down)
        x = jnp.concatenate([before, x, after], axis=dim)
    return x


def tap_weights(offsets):
    offsets_wide = offsets.astype(jnp.float32)
    tap_ids = jnp.arange(KN)
    tap_row = (tap_ids // 4).astype(jnp.float32)
    tap_col = (tap_ids % 4).astype(jnp.float32)
    delta_row = tap_row[None, :, None] - 1.5 - offsets_wide[:, 0:1, :]
    delta_col = tap_col[None, :, None] - 1.5 - offsets_wide[:, 1:2, :]
    return jnp.exp(-(delta_row * delta_row + delta_col * delta_col) * inverse_width).astype(
        jnp.bfloat16
    )


def kernel_matrix(cells, weights):
    slot_count, tap_count, obs_count = cells.shape
    slot_ids = jnp.broadcast_to(jnp.arange(slot_count, dtype=jnp.int32)[:, None, None], cells.shape)
    obs_ids = jnp.broadcast_to(jnp.arange(obs_count, dtype=jnp.int32)[None, None, :], cells.shape)
    blank = jnp.zeros((slot_count, PH * PW, obs_count), jnp.bfloat16)
    return blank.at[slot_ids, cells, obs_ids].set(weights)


def convolve(padded, weight, bias_vec):
    height = padded.shape[-3] - 2
    breadth = padded.shape[-2] - 2
    channels = padded.shape[-1]
    leading = padded.shape[:-3]
    summed = None
    for row_shift in range(3):
        rows_part = padded[..., row_shift : row_shift + height, :, :]
        stacked = jnp.concatenate(
            [rows_part[..., col_shift : col_shift + breadth, :] for col_shift in range(3)], axis=-1
        )
        product_term = jnp.dot(
            stacked.reshape(-1, 3 * channels),
            weight[row_shift].reshape(3 * channels, channels),
            preferred_element_type=jnp.float32,
        )
        summed = product_term if summed is None else summed + product_term
    return summed.reshape(leading + (height, breadth, channels)) + bias_vec


def grid_input(spread, density, density_weight):
    return (
        spread / jnp.maximum(density, 1.0)[..., None]
        + density_weight * (density / (1.0 + density))[..., None]
    ).astype(jnp.bfloat16)


def patches_to_tile(patches, tile_height, tile_width):
    trailing = patches.shape[2:]
    shaped = patches.reshape((tile_height // PH, tile_width // PW, PH, PW) + trailing)
    axes_order = (0, 2, 1, 3) + tuple(range(4, 4 + len(trailing)))
    return shaped.transpose(axes_order).reshape((tile_height, tile_width) + trailing)


def tile_to_patches(tile):
    tile_height, tile_width = (tile.shape[0], tile.shape[1])
    trailing = tile.shape[2:]
    shaped = tile.reshape((tile_height // PH, PH, tile_width // PW, PW) + trailing)
    axes_order = (0, 2, 1, 3) + tuple(range(4, 4 + len(trailing)))
    return shaped.transpose(axes_order).reshape(
        (tile_height // PH * (tile_width // PW), PH * PW) + trailing
    )


def plain_edges(stripe):
    return extended(stripe, ((("orbits", "rows"), 0), ("cols", 1)), 1)


def local(
    obs_feat,
    obs_offset,
    obs_cells,
    block_tile,
    block_patch,
    w_embed,
    b_embed,
    w_proj,
    b_proj,
    density_weight,
    w_first,
    b_first,
    w_second,
    b_second,
):
    channels = obs_feat.shape[1]
    block_count = block_tile.shape[0]
    block_size = obs_feat.shape[0] // block_count
    tiles = lax.axis_size("rows") * lax.axis_size("cols")
    orbit_count = lax.axis_size("orbits")
    most = max(2, 2 * block_count // tiles)
    slots = tiles * most
    tile_height = orbit_count * SR
    patch_count = tile_height // PH * (TC // PW)
    group_size = 16
    group_count = slots // group_size
    hidden = jax.nn.silu(
        jnp.dot(obs_feat, w_embed, preferred_element_type=jnp.float32) + b_embed
    ).astype(jnp.bfloat16)
    features = (jnp.dot(hidden, w_proj, preferred_element_type=jnp.float32) + b_proj).astype(
        jnp.bfloat16
    )
    positions = jnp.arange(block_count)
    same_tile = block_tile[:, None] == block_tile[None, :]
    earlier = positions[:, None] > positions[None, :]
    rank_in_tile = jnp.sum(same_tile & earlier, axis=1)
    slot_of = block_tile * most + rank_in_tile
    blocks = features.reshape(block_count, block_size, channels)
    send_feats = (
        jnp.zeros((slots, block_size, channels), jnp.bfloat16)
        .at[slot_of]
        .set(blocks)
        .reshape(tiles, most, block_size, channels)
    )
    local_offsets = obs_offset.reshape(2, block_count, block_size).transpose(1, 0, 2)
    send_offsets = (
        jnp.zeros((slots, 2, block_size), jnp.bfloat16)
        .at[slot_of]
        .set(local_offsets)
        .reshape(tiles, most, 2, block_size)
    )
    send_patch = jnp.full((slots,), -1, jnp.int32).at[slot_of].set(block_patch).reshape(tiles, most)
    local_cells = obs_cells.reshape(KN, block_count, block_size).transpose(1, 0, 2)
    send_cells = (
        jnp.zeros((slots, KN, block_size), jnp.int32)
        .at[slot_of]
        .set(local_cells)
        .reshape(tiles, most, KN, block_size)
    )
    got_feats, got_offsets, got_cells, got_patch = (
        lax.all_to_all(send_feats, ("rows", "cols"), split_axis=0, concat_axis=0, tiled=True),
        lax.all_to_all(send_offsets, ("rows", "cols"), split_axis=0, concat_axis=0, tiled=True),
        lax.all_to_all(send_cells, ("rows", "cols"), split_axis=0, concat_axis=0, tiled=True),
        lax.all_to_all(send_patch, ("rows", "cols"), split_axis=0, concat_axis=0, tiled=True),
    )
    got_cells = got_cells.reshape(slots, KN, block_size)
    got_feats = got_feats.reshape(slots, block_size, channels)
    got_offsets = got_offsets.reshape(slots, 2, block_size)
    got_patch = got_patch.reshape(slots)
    live = got_patch >= 0
    safe_patch = jnp.where(live, got_patch, 0)
    weights = tap_weights(got_offsets)
    live_weights = jnp.where(live[:, None, None], weights, jnp.zeros_like(weights))

    def regroup(array):
        return array.reshape((group_count, group_size) + array.shape[1:])

    patch_ids = jnp.arange(patch_count, dtype=jnp.int32)

    def spread_group(carry, parts):
        spread_sum, density_sum = carry
        feats_part, cells_part, weights_part, patch_part = parts
        matrix = kernel_matrix(cells_part, weights_part)
        contrib = jnp.einsum("sco,sod->scd", matrix, feats_part, preferred_element_type=jnp.float32)
        cell_weight = jnp.sum(matrix.astype(jnp.float32), axis=2)
        one_hot = (patch_part[None, :] == patch_ids[:, None]).astype(jnp.float32)
        spread_sum = spread_sum + jnp.einsum(
            "ps,scd->pcd", one_hot, contrib, precision=lax.Precision.HIGHEST
        )
        density_sum = density_sum + jnp.dot(one_hot, cell_weight, precision=lax.Precision.HIGHEST)
        return ((spread_sum, density_sum), None)

    start = (
        jnp.zeros((patch_count, PH * PW, channels), jnp.float32),
        jnp.zeros((patch_count, PH * PW), jnp.float32),
    )
    (spread_patches, density_patches), unused = lax.scan(
        spread_group,
        start,
        (regroup(got_feats), regroup(got_cells), regroup(live_weights), regroup(safe_patch)),
    )
    spread_tile = patches_to_tile(spread_patches, tile_height, TC)
    density_tile = patches_to_tile(density_patches, tile_height, TC)
    spread_part, density_part = (
        lax.psum_scatter(
            spread_tile.astype(jnp.bfloat16), "orbits", scatter_dimension=0, tiled=True
        ).astype(jnp.float32),
        lax.psum_scatter(
            density_tile.astype(jnp.bfloat16), "orbits", scatter_dimension=0, tiled=True
        ).astype(jnp.float32),
    )
    grid_in = grid_input(spread_part, density_part, density_weight)
    first = jax.nn.silu(convolve(plain_edges(grid_in), w_first, b_first)).astype(jnp.bfloat16)
    grid_out = (
        grid_in.astype(jnp.float32) + convolve(plain_edges(first), w_second, b_second)
    ).astype(jnp.bfloat16)
    full_out = lax.all_gather(grid_out, "orbits", axis=0, tiled=True)
    tile_values = tile_to_patches(full_out)

    def read_group(carry, parts):
        cells_part, weights_part, patch_part = parts
        matrix = kernel_matrix(cells_part, weights_part)
        values = tile_values[patch_part]
        summed = jnp.einsum("sco,scd->sod", matrix, values, preferred_element_type=jnp.float32)
        tap_total = jnp.sum(weights_part.astype(jnp.float32), axis=1)
        return (carry, (summed / tap_total[:, :, None]).astype(jnp.bfloat16))

    unused_carry, readings = lax.scan(
        read_group, 0, (regroup(got_cells), regroup(weights), regroup(safe_patch))
    )
    returned = lax.all_to_all(
        readings.reshape(tiles, most, block_size, channels),
        ("rows", "cols"),
        split_axis=0,
        concat_axis=0,
        tiled=True,
    )
    mine = returned.reshape(slots, block_size, channels)[slot_of].reshape(
        block_count * block_size, channels
    )
    obs_out = (features.astype(jnp.float32) + mine.astype(jnp.float32)).astype(jnp.bfloat16)
    return (obs_out, grid_out)


def solution(mesh):
    in_specs = (
        P(("orbits", "rows", "cols"), None),
        P(None, ("orbits", "rows", "cols")),
        P(None, ("orbits", "rows", "cols")),
        P(("orbits", "rows", "cols")),
        P(("orbits", "rows", "cols")),
        P(),
        P(),
        P(),
        P(),
        P(),
        P(),
        P(),
        P(),
        P(),
    )
    out_specs = (P(("orbits", "rows", "cols"), None), P(("orbits", "rows"), "cols", None))
    return jax.shard_map(local, mesh=mesh, in_specs=in_specs, out_specs=out_specs, check_vma=False)
```

profile of v0, /device:TPU:2, one launch (start us, length us, event | category | flops | bytes accessed | tf_op | source)
XLA Modules:
  0.0 2133.4 jit_solution(8321130745761410371)
XLA Ops:
  10.3 7.6 all-to-all-start.2
  18.6 3.7 scatter_fusion.1
  24.1 5.6 all-to-all-start.1
  31.5 3.9 scatter_fusion
  35.9 6.9 all-to-all-start
  45.5 4.6 scatter_fusion.2
  50.1 3.1 all-to-all-done
  53.2 6.1 all-to-all-start.3
  61.3 25.5 %all-to-all-done.3 = bf16[32,2,128,128]{3,2,1,0:T(8,128)(2,1)} async-done(((bf16[32,2,128,128]{3,2,1,0:T(8,128)(2,1)}), bf16[32,2,128,128]{3,2,1,0:T(8,128)(2,1)}, u32[]{:S(2)}, u32[]{:S(2)}) %all-to-all-start.3) | async-done | bytes 2097184 | tf_op jit(solution)/shard_map/all_to_all | solution.py:158
  86.7 947.7 %while.24 = (s32[]{:T(128)}, f32[32,256,128]{2,0,1:T(8,128)}, f32[32,256]{1,0:T(8,128)S(1)}, s32[4,16]{1,0:T(4,128)S(1)}, s32[4,16,16,128]{3,2,1,0:T(8,128)}, /*...) while((s32[]{:T(128)}, f32[32,256,128]{2,0,1:T(8,128)}, ...), condition=%wide.region_8.9_spmd.clone, body=%wide.region_5.8_spmd.clone.sunk | while | flops 341324800 | bytes 18252708 | solution.py:194
  88.0 224.7 %scatter_custom_fusion.17 = bf16[524288]{0:T(1024)(128)(2,1)S(1)} fusion(s32[32768]{0:T(1024)S(1)} %bitcast.152, bf16[32768]{0:T(1024)(128)(2,1)S(1)} %bitcast.156, bf16[]{:T(256)} %constant.97.clone.1..sunk.1), kind=kCustom, calls=%fused_computation.33.clone.1 | custom fusion | bytes 1048578 | tf_op jit(solution)/shard_map/while
  312.7 2.8 fusion.96
  315.5 6.5 select_add_fusion.2
  324.0 224.7 %scatter_custom_fusion.17 = bf16[524288]{0:T(1024)(128)(2,1)S(1)} fusion(s32[32768]{0:T(1024)S(1)} %bitcast.152, bf16[32768]{0:T(1024)(128)(2,1)S(1)} %bitcast.156, bf16[]{:T(256)} %constant.97.clone.1..sunk.1), kind=kCustom, calls=%fused_computation.33.clone.1 | custom fusion | bytes 1048578 | tf_op jit(solution)/shard_map/while
  548.7 2.8 fusion.96
  551.6 7.8 select_add_fusion.2
  561.2 224.7 %scatter_custom_fusion.17 = bf16[524288]{0:T(1024)(128)(2,1)S(1)} fusion(s32[32768]{0:T(1024)S(1)} %bitcast.152, bf16[32768]{0:T(1024)(128)(2,1)S(1)} %bitcast.156, bf16[]{:T(256)} %constant.97.clone.1..sunk.1), kind=kCustom, calls=%fused_computation.33.clone.1 | custom fusion | bytes 1048578 | tf_op jit(solution)/shard_map/while
  786.0 2.8 fusion.96
  788.8 7.8 select_add_fusion.2
  798.5 224.7 %scatter_custom_fusion.17 = bf16[524288]{0:T(1024)(128)(2,1)S(1)} fusion(s32[32768]{0:T(1024)S(1)} %bitcast.152, bf16[32768]{0:T(1024)(128)(2,1)S(1)} %bitcast.156, bf16[]{:T(256)} %constant.97.clone.1..sunk.1), kind=kCustom, calls=%fused_computation.33.clone.1 | custom fusion | bytes 1048578 | tf_op jit(solution)/shard_map/while
  1023.2 2.8 fusion.96
  1026.0 7.8 select_add_fusion.2
  1035.4 2.7 convert_element_type.107
  1038.1 2.7 copy.40
  1040.9 16.1 reduce-scatter.5.cloned.1.call-done
  1057.6 31.3 %reduce-scatter.3.cloned.1.call-done = bf16[16,128,128]{2,1,0:T(8,128)(2,1)} async-done(((bf16[64,128,128]{2,1,0:T(8,128)(2,1)}), bf16[16,128,128]{2,1,0:T(8,128)(2,1)}) %reduce-scatter.3.cloned.1.call-update) | async-done | bytes 524304 | tf_op jit(solution)/shard_map/reduce_scatter | solution.py:202
  1090.6 1.9 collective-permute-start
  1092.5 3.6 collective-permute-start.1
  1097.8 3.4 collective-permute-start.2
  1102.7 4.0 collective-permute-done.3
  1110.7 2.0 collective-permute-start.4
  1112.8 3.5 collective-permute-start.5
  1117.9 3.4 collective-permute-start.6
  1122.7 4.2 collective-permute-done.7
  1132.7 32.0 %all-gather.2.cloned.1.call-done = bf16[64,128,128]{2,1,0:T(8,128)(2,1)} async-done(((bf16[16,128,128]{2,1,0:T(8,128)(2,1)}), bf16[64,128,128]{2,1,0:T(8,128)(2,1)}) %all-gather.2.cloned.1.call-update) | async-done | bytes 2097168 | tf_op jit(solution)/shard_map/all_gather | solution.py:214
  1164.7 3.5 copy.42
  1168.2 919.6 %while.23 = (s32[]{:T(128)}, bf16[4,16,128,128]{3,2,1,0:T(8,128)(2,1)}, s32[4,16,16,128]{3,2,1,0:T(8,128)}, bf16[4,16,16,128]{3,2,1,0:T(8,128)(2,1)S(1)}, s32[4,...) while((s32[]{:T(128)}, ...), condition=%wide.region_14.15_spmd, body=%wide.region_11.14_spmd.sunk | while | flops 135855152 | bytes 7689099 | solution.py:225
  1169.4 224.7 %scatter_custom_fusion.15 = bf16[524288]{0:T(1024)(128)(2,1)S(1)} fusion(s32[32768]{0:T(1024)S(1)} %bitcast.151, bf16[32768]{0:T(1024)(128)(2,1)S(1)} %bitcast.155, bf16[]{:T(256)} %constant.97.clone.1..sunk), kind=kCustom, calls=%fused_computation.13.clone.1 | custom fusion | bytes 1048578 | tf_op jit(solution)/shard_map/while
  1394.2 2.3 gather_fusion
  1399.3 224.7 %scatter_custom_fusion.15 = bf16[524288]{0:T(1024)(128)(2,1)S(1)} fusion(s32[32768]{0:T(1024)S(1)} %bitcast.151, bf16[32768]{0:T(1024)(128)(2,1)S(1)} %bitcast.155, bf16[]{:T(256)} %constant.97.clone.1..sunk), kind=kCustom, calls=%fused_computation.13.clone.1 | custom fusion | bytes 1048578 | tf_op jit(solution)/shard_map/while
  1624.1 2.3 gather_fusion
  1629.2 224.7 %scatter_custom_fusion.15 = bf16[524288]{0:T(1024)(128)(2,1)S(1)} fusion(s32[32768]{0:T(1024)S(1)} %bitcast.151, bf16[32768]{0:T(1024)(128)(2,1)S(1)} %bitcast.155, bf16[]{:T(256)} %constant.97.clone.1..sunk), kind=kCustom, calls=%fused_computation.13.clone.1 | custom fusion | bytes 1048578 | tf_op jit(solution)/shard_map/while
  1854.0 2.3 gather_fusion
  1859.1 224.7 %scatter_custom_fusion.15 = bf16[524288]{0:T(1024)(128)(2,1)S(1)} fusion(s32[32768]{0:T(1024)S(1)} %bitcast.151, bf16[32768]{0:T(1024)(128)(2,1)S(1)} %bitcast.155, bf16[]{:T(256)} %constant.97.clone.1..sunk), kind=kCustom, calls=%fused_computation.13.clone.1 | custom fusion | bytes 1048578 | tf_op jit(solution)/shard_map/while
  2083.9 2.3 gather_fusion
  2087.7 7.4 all-to-all-start.4
  2095.2 27.2 %all-to-all-done.4 = bf16[32,2,128,128]{3,2,1,0:T(8,128)(2,1)S(1)} async-done(((bf16[32,2,128,128]{3,2,1,0:T(8,128)(2,1)}), bf16[32,2,128,128]{3,2,1,0:T(8,128)(2,1)S(1)}, u32[]{:S(2)}, u32[]{:S(2)}) %all-to-all-start.4) | async-done | bytes 2097184 | tf_op jit(solution)/shard_map/all_to_all | solution.py:228
  2124.1 2.8 fusion.22
  (176 shorter events, 51.5 us)
Async XLA Ops:
  7.2 35.6 %copy-start = (bf16[4096,128]{1,0:T(8,128)(2,1)S(1)}, bf16[4096,128]{1,0:T(8,128)(2,1)}, u32[]{:S(2)}) copy-start(bf16[4096,128]{1,0:T(8,128)(2,1)} %param.18) | copy-start | bytes 3145732
  7.2 35.6 %copy-start.11 = (bf16[128,128]{1,0:T(8,128)(2,1)S(1)}, bf16[128,128]{1,0:T(8,128)(2,1)}, u32[]{:S(2)}) copy-start(bf16[128,128]{1,0:T(8,128)(2,1)} %param.23) | copy-start | bytes 98308
  7.2 35.6 %copy-start.13 = (f32[128]{0:T(128)S(1)}, f32[128]{0:T(128)}, u32[]{:S(2)}) copy-start(f32[128]{0:T(128)} %param.24) | copy-start | bytes 1540
  7.2 35.6 %copy-start.10 = (bf16[128,128]{1,0:T(8,128)(2,1)S(1)}, bf16[128,128]{1,0:T(8,128)(2,1)}, u32[]{:S(2)}) copy-start(bf16[128,128]{1,0:T(8,128)(2,1)} %param.25) | copy-start | bytes 98308
  7.2 35.6 %copy-start.12 = (f32[128]{0:T(128)S(1)}, f32[128]{0:T(128)}, u32[]{:S(2)}) copy-start(f32[128]{0:T(128)} %param.26) | copy-start | bytes 1540
  10.3 13.7 all-to-all-start.2
  24.1 11.8 all-to-all-start.1
  35.9 17.4 all-to-all-start
  43.6 6.5 copy-start.1
  53.2 33.5 %copy-start.5 = (s32[3]{0:T(128)S(1)}, s32[3]{0:T(128)}, u32[]{:S(2)}) copy-start(s32[3]{0:T(128)} %constant.226) | copy-start | bytes 40
  53.2 33.5 %copy-start.6 = (s32[3]{0:T(128)S(1)}, s32[3]{0:T(128)}, u32[]{:S(2)}) copy-start(s32[3]{0:T(128)} %constant.227) | copy-start | bytes 40
  53.2 33.5 %all-to-all-start.3 = ((bf16[32,2,128,128]{3,2,1,0:T(8,128)(2,1)}), bf16[32,2,128,128]{3,2,1,0:T(8,128)(2,1)}, u32[]{:S(2)}, u32[]{:S(2)}) async-start(bf16[32,2,128,128]{3,2,1,0:T(8,128)(2,1)} %bitcast.19), calls=%async_computation.3 | async-start | bytes 4194304 | tf_op jit(solution)/shard_map/all_to_all | solution.py:158
  59.3 997.6 %reduce-scatter.5.cloned.1.call-start = ((), (), s32[]{:S(2)}) async-start(), calls=%async_computation.8 | async-start | bytes 20480 | tf_op jit(solution)/shard_map/reduce_scatter | solution.py:205
  1035.3 53.5 %reduce-scatter.3.cloned.1.call-start = ((), (), s32[]{:S(2)}) async-start(), calls=%async_computation.7 | async-start | bytes 2621440 | tf_op jit(solution)/shard_map/reduce_scatter | solution.py:202
  1040.8 48.1 %copy-start.7 = (f32[128]{0:T(128)S(1)}, f32[128]{0:T(128)}, u32[]{:S(2)}) copy-start(f32[128]{0:T(128)} %param.27) | copy-start | bytes 1540
  1040.8 61.9 %copy-start.3 = (bf16[3,3,128,128]{3,2,1,0:T(8,128)(2,1)S(1)}, bf16[3,3,128,128]{3,2,1,0:T(8,128)(2,1)}, u32[]{:S(2)}) copy-start(bf16[3,3,128,128]{3,2,1,0:T(8,128)(2,1)} %param.28) | copy-start | bytes 884740
  1040.8 123.9 %all-gather.2.cloned.1.call-start = ((), (), s32[]{:S(2)}) async-start(), calls=%async_computation.9 | async-start | bytes 2621440 | tf_op jit(solution)/shard_map/all_gather | solution.py:214
  1090.6 5.6 collective-permute-start
  1092.5 5.2 collective-permute-start.1
  1097.8 5.0 collective-permute-start.2
  1101.2 5.6 collective-permute-start.3
  1109.8 0.7 copy-start.8
  1110.4 12.2 copy-start.4
  1110.7 5.6 collective-permute-start.4
  1112.8 5.1 collective-permute-start.5
  1117.9 4.7 collective-permute-start.6
  1121.3 5.6 collective-permute-start.7
  1129.9 1.0 copy-start.2
  1130.0 1.0 copy-start.9
  2087.7 34.7 %all-to-all-start.4 = ((bf16[32,2,128,128]{3,2,1,0:T(8,128)(2,1)}), bf16[32,2,128,128]{3,2,1,0:T(8,128)(2,1)S(1)}, u32[]{:S(2)}, u32[]{:S(2)}) async-start(bf16[32,2,128,128]{3,2,1,0:T(8,128)(2,1)} %bitcast.153), calls=%async_computation.6 | async-start | bytes 4194304 | tf_op jit(solution)/shard_map/all_to_all | solution.py:228
Sparse Core Ops, SparseCore 0:
  1035.5 21.4 reduce-scatter.4
  1059.3 29.5 reduce-scatter.2
  1132.5 32.0 all-gather.1
where the time goes:
time: 2140 us; the launch traced here: 2130 us
  local copies, waits for them, and re-layouts  1840 us (86%)
  waiting for transfers between devices  149 us (7%)
  starting transfers between devices  54.6 us (3%)
  matrix products  52.6 us (2%)
  other arithmetic  25.6 us (1%)
    while x8, local copies, waits for them, and re-layouts  1800 us
  transfers between devices with their start and end apart: 16, of which 12 were waited for; matrix products, arithmetic and copies ran while one was open for 1% of the time, Pallas kernels for 0%

commit v1 on v0

v1 whole, which is shorter than its diff:
```python
import functools

import jax
import jax.numpy as jnp
from jax import lax
from jax.experimental import pallas as pl
from jax.experimental.pallas import tpu as pltpu
from jax.sharding import PartitionSpec as P

KN = 16
PH = 8
PW = 32
SR = 16
TC = 128
BLK = 128
C = 128
MOST = 2
PAIR = MOST * BLK + 16
MESH = pl.DeviceIdType.MESH
VMEM = pltpu.VMEM
SMEM = pltpu.SMEM


def plane_device(index, cols):
    return (lax.axis_index("orbits"), index // cols, index % cols)


def plane_barrier(me, tiles, cols):
    barrier = pltpu.get_barrier_semaphore()

    def greet(k, carry):
        pl.semaphore_signal(barrier, inc=1, device_id=plane_device((me + k) % tiles, cols), device_id_type=MESH)
        return carry

    lax.fori_loop(1, tiles, greet, 0)
    pl.semaphore_wait(barrier, tiles - 1)


def window_weights(meta_rows):
    off_r, off_c = meta_rows[0:1], meta_rows[1:2]
    anchor_r, anchor_c = meta_rows[2:3], meta_rows[3:4]
    tap_r = lax.broadcasted_iota(jnp.int32, (PH, BLK), 0).astype(jnp.float32) - anchor_r
    tap_c = lax.broadcasted_iota(jnp.int32, (PW, BLK), 0).astype(jnp.float32) - anchor_c
    delta_r = tap_r - 1.5 - off_r
    delta_c = tap_c - 1.5 - off_c
    weight_r = jnp.where((tap_r >= 0.0) & (tap_r < 4.0), jnp.exp(delta_r * delta_r * -0.5), 0.0)
    weight_c = jnp.where((tap_c >= 0.0) & (tap_c < 4.0), jnp.exp(delta_c * delta_c * -0.5), 0.0)
    return jnp.concatenate([(weight_r[r : r + 1] * weight_c).astype(jnp.bfloat16) for r in range(PH)], axis=0)


def scatter_kernel(
    tiles, cols, blocks, block_ref, patch_ref, feat_ref, off_ref, cells_ref, we_ref, be_ref, wp_ref, bp_ref,
    features_ref, got_ref, send, block_meta, send_sem, recv_sem, own_sem,
):
    me = lax.axis_index("rows") * cols + lax.axis_index("cols")
    plane_barrier(me, tiles, cols)
    group = min(4, blocks)

    def embed(i, carry):
        rows = pl.ds(i * group, group)
        x = feat_ref[rows].reshape(group * BLK, C)
        v = jnp.dot(x, we_ref[...], preferred_element_type=jnp.float32) + be_ref[...]
        hidden = (v / (1.0 + jnp.exp(-v))).astype(jnp.bfloat16)
        out = jnp.dot(hidden, wp_ref[...], preferred_element_type=jnp.float32) + bp_ref[...]
        features_ref[rows] = out.astype(jnp.bfloat16).reshape(group, BLK, C)
        return carry

    lax.fori_loop(0, blocks // group, embed, 0)
    row_id = lax.broadcasted_iota(jnp.int32, (8, BLK), 0)
    for b in range(blocks):
        lanes = slice(b * BLK, (b + 1) * BLK)
        off = off_ref[:, lanes].astype(jnp.float32)
        cell = cells_ref[0:1, lanes]
        meta = jnp.where(row_id == 0, off[0:1], 0.0)
        meta = jnp.where(row_id == 1, off[1:2], meta)
        meta = jnp.where(row_id == 2, (cell >> 5).astype(jnp.float32), meta)
        block_meta[b] = jnp.where(row_id == 3, (cell & 31).astype(jnp.float32), meta)

    def out_copy(t):
        return pltpu.make_async_remote_copy(
            src_ref=send.at[t], dst_ref=got_ref.at[me], send_sem=send_sem.at[t], recv_sem=recv_sem.at[me],
            device_id=plane_device(t, cols), device_id_type=MESH,
        )

    def in_copy(s):
        return pltpu.make_async_remote_copy(
            src_ref=send.at[s], dst_ref=got_ref.at[s], send_sem=send_sem.at[s], recv_sem=recv_sem.at[s],
            device_id=plane_device(s, cols), device_id_type=MESH,
        )

    def pack(t):
        metas = []
        for j in range(MOST):
            slot = t * MOST + j
            block = block_ref[slot]
            patch = jnp.full((8, BLK), patch_ref[slot].astype(jnp.float32))
            send[t, j * BLK : (j + 1) * BLK, :] = features_ref[block]
            meta = block_meta[block]
            meta = jnp.where((row_id == 2) & (patch < 0.0), -100.0, meta)
            metas.append(jnp.where(row_id == 4, patch, meta))
        send[t, MOST * BLK :, :] = jnp.concatenate(metas, axis=0).astype(jnp.bfloat16)

    def start_one(k, carry):
        t = (me + k) % tiles
        pack(t)
        out_copy(t).start()
        return carry

    lax.fori_loop(1, tiles, start_one, 0)
    pack(me)
    own = pltpu.make_async_copy(send.at[me], got_ref.at[me], own_sem)
    own.start()
    own.wait()

    def finish(k, carry):
        out_copy((me + k) % tiles).wait_send()
        in_copy((me + tiles - k) % tiles).wait_recv()
        return carry

    lax.fori_loop(1, tiles, finish, 0)


def spread_kernel(tiles, patches, patch_ref, got_ref, spread_ref, density_ref, acc, density_acc):
    step = pl.program_id(0)

    @pl.when(step == 0)
    def _():
        acc[...] = jnp.zeros_like(acc)
        density_acc[...] = jnp.zeros_like(density_acc)

    metas = got_ref[0, MOST * BLK :, :].astype(jnp.float32)
    ones = jnp.ones((8, BLK), jnp.bfloat16)
    for j in range(MOST):
        patch = patch_ref[step * MOST + j]

        @pl.when(patch >= 0)
        def _():
            matrix = window_weights(metas[8 * j : 8 * j + 8])
            acc[patch] += jnp.dot(matrix, got_ref[0, j * BLK : (j + 1) * BLK, :], preferred_element_type=jnp.float32)
            sums = lax.dot_general(ones, matrix, (((1,), (1,)), ((), ())), preferred_element_type=jnp.float32)
            density_acc[pl.ds(patch, 1), :] += sums[0:1]

    @pl.when(step == tiles - 1)
    def _():
        spread_ref[...] = acc[...].astype(jnp.bfloat16)
        density_ref[...] = density_acc[...].astype(jnp.bfloat16)


def read_kernel(
    tiles, cols, blocks, patch_ref, slot_ref, meta_ref, tile_ref, features_ref,
    out_ref, values_ref, send, got, send_sem, recv_sem,
):
    me = lax.axis_index("rows") * cols + lax.axis_index("cols")
    plane_barrier(me, tiles, cols)
    across = TC // PW
    for p in range(values_ref.shape[0]):
        top, left = p // across * PH, p % across * PW
        values_ref[p] = tile_ref[top : top + PH, left : left + PW, :].reshape(PH * PW, C)
    ones = jnp.ones((PH * PW, C), jnp.bfloat16)

    def pair(t):
        return pl.ds(t * MOST, MOST)

    def out_copy(t):
        return pltpu.make_async_remote_copy(
            src_ref=send.at[pair(t)], dst_ref=got.at[pair(me)], send_sem=send_sem.at[t], recv_sem=recv_sem.at[me],
            device_id=plane_device(t, cols), device_id_type=MESH,
        )

    def in_copy(s):
        return pltpu.make_async_remote_copy(
            src_ref=send.at[pair(s)], dst_ref=got.at[pair(s)], send_sem=send_sem.at[s], recv_sem=recv_sem.at[s],
            device_id=plane_device(s, cols), device_id_type=MESH,
        )

    def read(s, target):
        metas = meta_ref[s].astype(jnp.float32)
        for j in range(MOST):
            rows = metas[8 * j : 8 * j + 8]
            row_id = lax.broadcasted_iota(jnp.int32, (8, BLK), 0)
            rows = jnp.where((row_id == 2) & (rows < 0.0), 0.0, rows)
            matrix = window_weights(rows)
            both = jnp.concatenate([values_ref[patch_ref[s * MOST + j]], ones], axis=1)
            summed = lax.dot_general(matrix, both, (((0,), (0,)), ((), ())), preferred_element_type=jnp.float32)
            target[s * MOST + j] = (summed[:, :C] / summed[:, C:]).astype(jnp.bfloat16)

    def start_one(k, carry):
        s = (me + k) % tiles
        read(s, send)
        out_copy(s).start()
        return carry

    lax.fori_loop(1, tiles, start_one, 0)
    read(me, got)

    def finish(k, carry):
        out_copy((me + k) % tiles).wait_send()
        in_copy((me + tiles - k) % tiles).wait_recv()
        return carry

    lax.fori_loop(1, tiles, finish, 0)

    def combine(b, carry):
        reading = got[slot_ref[b]]
        out_ref[b] = (features_ref[b].astype(jnp.float32) + reading.astype(jnp.float32)).astype(jnp.bfloat16)
        return carry

    lax.fori_loop(0, blocks, combine, 0)


def extended(x, sides, width):
    for axis, dim in sides:
        size, length = (lax.axis_size(axis), x.shape[dim])
        up = [(i, (i + 1) % size) for i in range(size - 1)]
        down = [(j, i) for i, j in up]
        last = lax.slice_in_dim(x, length - width, length, axis=dim)
        initial = lax.slice_in_dim(x, 0, width, axis=dim)
        before = lax.ppermute(last, axis, up)
        after = lax.ppermute(initial, axis, down)
        x = jnp.concatenate([before, x, after], axis=dim)
    return x


def convolve(padded, weight, bias_vec):
    height = padded.shape[-3] - 2
    breadth = padded.shape[-2] - 2
    channels = padded.shape[-1]
    summed = None
    for row_shift in range(3):
        rows_part = padded[row_shift : row_shift + height]
        stacked = jnp.concatenate([rows_part[:, s : s + breadth, :] for s in range(3)], axis=-1)
        term = jnp.dot(
            stacked.reshape(-1, 3 * channels), weight[row_shift].reshape(3 * channels, channels),
            preferred_element_type=jnp.float32,
        )
        summed = term if summed is None else summed + term
    return summed.reshape((height, breadth, channels)) + bias_vec


def patches_to_tile(patches, tile_height, tile_width):
    trailing = patches.shape[2:]
    shaped = patches.reshape((tile_height // PH, tile_width // PW, PH, PW) + trailing)
    axes_order = (0, 2, 1, 3) + tuple(range(4, 4 + len(trailing)))
    return shaped.transpose(axes_order).reshape((tile_height, tile_width) + trailing)


def plain_edges(stripe):
    return extended(stripe, ((("orbits", "rows"), 0), ("cols", 1)), 1)


def local(
    obs_feat, obs_offset, obs_cells, block_tile, block_patch, w_embed, b_embed, w_proj, b_proj, density_weight,
    w_first, b_first, w_second, b_second,
):
    blocks = block_tile.shape[0]
    cols = lax.axis_size("cols")
    tiles = lax.axis_size("rows") * cols
    orbits = lax.axis_size("orbits")
    tile_height = orbits * SR
    patches = tile_height // PH * (TC // PW)
    slots = tiles * MOST

    ids = jnp.arange(blocks, dtype=jnp.int32)
    tile_ids = jnp.arange(tiles, dtype=jnp.int32)
    hit = block_tile[None, :] == tile_ids[:, None]
    lowest = jnp.min(jnp.where(hit, ids[None, :], blocks), axis=1)
    highest = jnp.max(jnp.where(hit, ids[None, :], -1), axis=1)
    block_of_slot = jnp.stack([jnp.where(highest >= 0, lowest, -1), jnp.where(highest > lowest, highest, -1)], axis=1).reshape(slots)
    patch_at = jnp.sum(jnp.where(block_of_slot[:, None] == ids[None, :], block_patch[None, :] + 1, 0), axis=1) - 1
    later = jnp.any((block_tile[:, None] == block_tile[None, :]) & (ids[:, None] > ids[None, :]), axis=1)
    slot_of = block_tile * MOST + later.astype(jnp.int32)

    vm = pl.BlockSpec(memory_space=VMEM)
    sm = pl.BlockSpec(memory_space=SMEM)
    anyspace = pl.BlockSpec(memory_space=pl.ANY)
    features, got = pl.pallas_call(
        functools.partial(scatter_kernel, tiles, cols, blocks),
        grid=(1,),
        out_shape=(
            jax.ShapeDtypeStruct((blocks, BLK, C), jnp.bfloat16),
            jax.ShapeDtypeStruct((tiles, PAIR, C), jnp.bfloat16),
        ),
        in_specs=[sm, sm, vm, vm, pl.BlockSpec((8, blocks * BLK), lambda i: (0, 0)), vm, vm, vm, vm],
        out_specs=(vm, anyspace),
        scratch_shapes=[
            VMEM((tiles, PAIR, C), jnp.bfloat16),
            VMEM((blocks, 8, BLK), jnp.float32),
            pltpu.SemaphoreType.DMA((tiles,)),
            pltpu.SemaphoreType.DMA((tiles,)),
            pltpu.SemaphoreType.DMA,
        ],
        compiler_params=pltpu.CompilerParams(collective_id=0, has_side_effects=True),
        name="embed_and_send",
    )(jnp.maximum(block_of_slot, 0), patch_at, obs_feat.reshape(blocks, BLK, C), obs_offset, obs_cells, w_embed, b_embed[None, :], w_proj, b_proj[None, :])

    got_patch = jnp.stack([got[:, MOST * BLK + 4, 0], got[:, MOST * BLK + 12, 0]], axis=1).astype(jnp.int32).reshape(slots)

    spread, density = pl.pallas_call(
        functools.partial(spread_kernel, tiles, patches),
        grid_spec=pltpu.PrefetchScalarGridSpec(
            num_scalar_prefetch=1,
            grid=(tiles,),
            in_specs=[pl.BlockSpec((1, PAIR, C), lambda i, p: (i, 0, 0))],
            out_specs=(
                pl.BlockSpec((patches, PH * PW, C), lambda i, p: (0, 0, 0)),
                pl.BlockSpec((patches, PH * PW), lambda i, p: (0, 0)),
            ),
            scratch_shapes=[VMEM((patches, PH * PW, C), jnp.float32), VMEM((patches, PH * PW), jnp.float32)],
        ),
        out_shape=(
            jax.ShapeDtypeStruct((patches, PH * PW, C), jnp.bfloat16),
            jax.ShapeDtypeStruct((patches, PH * PW), jnp.bfloat16),
        ),
        name="spread",
    )(got_patch, got)

    spread_tile = patches_to_tile(spread, tile_height, TC)
    density_tile = patches_to_tile(density, tile_height, TC)
    spread_part = lax.psum_scatter(spread_tile, "orbits", scatter_dimension=0, tiled=True).astype(jnp.float32)
    density_part = lax.psum_scatter(density_tile, "orbits", scatter_dimension=0, tiled=True).astype(jnp.float32)
    grid_in = (
        spread_part / jnp.maximum(density_part, 1.0)[..., None]
        + density_weight * (density_part / (1.0 + density_part))[..., None]
    ).astype(jnp.bfloat16)
    first = jax.nn.silu(convolve(plain_edges(grid_in), w_first, b_first)).astype(jnp.bfloat16)
    grid_out = (grid_in.astype(jnp.float32) + convolve(plain_edges(first), w_second, b_second)).astype(jnp.bfloat16)
    full_out = lax.all_gather(grid_out, "orbits", axis=0, tiled=True)

    obs_out = pl.pallas_call(
        functools.partial(read_kernel, tiles, cols, blocks),
        grid=(1,),
        out_shape=jax.ShapeDtypeStruct((blocks, BLK, C), jnp.bfloat16),
        in_specs=[sm, sm, pl.BlockSpec((tiles, 16, C), lambda i: (0, MOST * BLK // 16, 0)), vm, vm],
        out_specs=vm,
        scratch_shapes=[
            VMEM((patches, PH * PW, C), jnp.bfloat16),
            VMEM((slots, BLK, C), jnp.bfloat16),
            VMEM((slots, BLK, C), jnp.bfloat16),
            pltpu.SemaphoreType.DMA((tiles,)),
            pltpu.SemaphoreType.DMA((tiles,)),
        ],
        compiler_params=pltpu.CompilerParams(collective_id=1, has_side_effects=True),
        name="read_and_return",
    )(jnp.maximum(got_patch, 0), slot_of, got, full_out, features)
    return (obs_out.reshape(obs_feat.shape), grid_out)


def solution(mesh):
    spread_out = P(("orbits", "rows", "cols"), None)
    in_specs = (
        spread_out, P(None, ("orbits", "rows", "cols")), P(None, ("orbits", "rows", "cols")),
        P(("orbits", "rows", "cols")), P(("orbits", "rows", "cols")),
        P(), P(), P(), P(), P(), P(), P(), P(), P(),
    )
    out_specs = (spread_out, P(("orbits", "rows"), "cols", None))
    return jax.shard_map(local, mesh=mesh, in_specs=in_specs, out_specs=out_specs, check_vma=False)
```

time: 2140 us -> 258 us (0.12)
  local copies, waits for them, and re-layouts: 1840 us -> 11.4 us
  Pallas kernels: 0 us -> 98.1 us
  waiting for transfers between devices: 149 us -> 96.5 us
  matrix products: 52.6 us -> 3.48 us
  starting transfers between devices: 54.6 us -> 20.6 us
    while x8 -> x0, local copies, waits for them, and re-layouts: 1800 us -> none
    pallas_call x0 -> x3, Pallas kernels: none -> 98.1 us  [the longest x1 42 us: local(): pl.pallas_call(functools.partial(scatter_kernel, tiles, cols, blocks), gr...]
    all_to_all x5 -> x0, waiting for transfers between devices: 58.1 us -> none  [the longest x1 27.2 us: local(): lax.all_to_all(readings.reshape(tiles, most, block_size, channels), ('row...]
    dot_general x17 -> x0, matrix products: 49.1 us -> none  [the longest x4 29.8 us: spread_group(): jnp.einsum('ps,scd->pcd', one_hot, contrib, precision=lax.Precision.HIGHEST)]
    all_to_all x5 -> x0, starting transfers between devices: 33.6 us -> none  [the longest x1 7.62 us: local(): lax.all_to_all(send_patch, ('rows', 'cols'), split_axis=0, concat_axis=0,...]
  transfers between devices with their start and end apart: 16 -> 11, of which waited for: 12 -> 7; matrix products, arithmetic and copies ran while one was open for 1% -> 2% of each run, Pallas kernels for 0% -> 0%
where the time goes in v1:
time: 258 us; the launch traced here: 254 us
  Pallas kernels  98.1 us (38%)
  waiting for transfers between devices  96.5 us (37%)
  starting transfers between devices  20.6 us (8%)
  between operations  14.1 us (5%)
  local copies, waits for them, and re-layouts  11.4 us (4%)
  other arithmetic  9.67 us (4%)
  matrix products  3.48 us (1%)
    pallas_call x1, Pallas kernels, local(): pl.pallas_call(functools.partial(scatter_kernel, tiles, cols, blocks), gr...  42 us
    pallas_call x1, Pallas kernels, local(): pl.pallas_call(functools.partial(read_kernel, tiles, cols, blocks), grid=...  35.3 us
    reduce_scatter x1, waiting for transfers between devices, local(): lax.psum_scatter(spread_tile, 'orbits', scatter_dimension=0, tiled=True)  31.3 us
    all_gather x1, waiting for transfers between devices, local(): full_out = lax.all_gather(grid_out, 'orbits', axis=0, tiled=True)  31 us
    reduce_scatter x1, waiting for transfers between devices, local(): lax.psum_scatter(density_tile, 'orbits', scatter_dimension=0, tiled=True)  22.7 us
    pallas_call x1, Pallas kernels, local(): pl.pallas_call(functools.partial(spread_kernel, tiles, patches), grid_spe...  20.8 us
    ppermute x4, waiting for transfers between devices, extended(): after = lax.ppermute(initial, axis, down)  11.5 us
    ppermute x4, starting transfers between devices, extended(): before = lax.ppermute(last, axis, up)  10.7 us
  transfers between devices with their start and end apart: 11, of which 7 were waited for; matrix products, arithmetic and copies ran while one was open for 2% of the time, Pallas kernels for 0%

profile of v1, /device:TPU:2, one launch (start us, length us, event | category | flops | bytes accessed | tf_op | source)
XLA Modules:
  0.0 253.9 jit_solution(16754537930158178662)
XLA Ops:
  7.2 0.8 select_reduce_fusion.2
  8.2 0.7 broadcast_add_fusion.1
  9.0 0.5 broadcast_add_fusion
  9.5 42.0 %embed_and_send.1 = (bf16[32,128,128]{2,1,0:T(8,128)(2,1)}, bf16[32,272,128]{2,1,0:T(8,128)(2,1)}) custom-call(s32[64]{0:T(128)} %get-tuple-element.55.block_ref, s32[64]{0:T(128)} %get-tuple-element.54.patch_ref, bf16[32,128,128]{2,1,0:T(8,128)(2,1)} %bitcast.56, bf16[2,4096]{1,0:T(2,128)(2,1)} %off_ref.1, s32[16,4096]{1,0:T(8,128)} %cells_ref.1, ...), custom_call_target="tpu_custom_call" | custom-call | tf_op jit(solution)/shard_map/embed_and_send/pallas_call | solution.py:276
  51.5 1.2 slice_reduce_fusion.1
  52.8 0.6 reshape.106.patch_ref
  53.4 20.8 %spread.1 = (bf16[32,256,128]{2,1,0:T(8,128)(2,1)}, bf16[32,256]{1,0:T(8,128)(2,1)}) custom-call(s32[64]{0:T(128)} %reshape.106.patch_ref, bf16[32,272,128]{2,1,0:T(8,128)(2,1)} %get-tuple-element.6.got_ref.meta_ref), custom_call_target="tpu_custom_call" | custom-call | tf_op jit(solution)/shard_map/spread/pallas_call | solution.py:298
  74.2 0.8 reshape.95
  75.0 0.7 reshape.96
  75.8 3.5 %copy.33 = bf16[8,8,4,32,128]{4,3,2,1,0:T(8,128)(2,1)} copy(bf16[8,8,4,32,128]{4,3,1,2,0:T(8,128)(2,1)} %bitcast.55) | data formatting | bytes 4194304 | tf_op jit(solution)/shard_map/transpose | solution.py:244
  79.4 22.7 %reduce-scatter.5.cloned.1.call-done = bf16[16,128]{1,0:T(8,128)(2,1)} async-done(((bf16[64,128]{1,0:T(8,128)(2,1)}), bf16[16,128]{1,0:T(8,128)(2,1)}) %reduce-scatter.5.cloned.1.call-update) | async-done | bytes 4112 | tf_op jit(solution)/shard_map/reduce_scatter | solution.py:320
  102.1 0.7 convert_maximum_fusion
  102.8 31.3 %reduce-scatter.3.cloned.1.call-done = bf16[16,128,128]{2,1,0:T(8,128)(2,1)} async-done(((bf16[64,128,128]{2,1,0:T(8,128)(2,1)}), bf16[16,128,128]{2,1,0:T(8,128)(2,1)}) %reduce-scatter.3.cloned.1.call-update) | async-done | bytes 524304 | tf_op jit(solution)/shard_map/reduce_scatter | solution.py:319
  134.0 1.7 add_convert_fusion.1
  135.7 1.9 collective-permute-start
  137.7 3.6 %collective-permute-start.1 = (bf16[1,128,128]{2,1,0:T(8,128)(2,1)S(1)}, bf16[1,128,128]{2,1,0:T(8,128)(2,1)S(1)}, u32[]{:S(2)}, u32[]{:S(2)}) collective-permute-start(bf16[1,128,128]{2,1,0:T(8,128)(2,1)S(1)} %get-tuple-element.42), channel_id=1, source_target_pairs={{4,0},{8,4},{12,8},{16,12},{20,16},{24,20},{28,24},{32,28},{36,32}... | collective-permute-start | bytes 98312 | tf_op jit(solution)/shard_map/ppermute | solution.py:219
  141.3 1.6 collective-permute-done.1
  142.9 3.4 %collective-permute-start.2 = (bf16[18,1,128]{2,1,0:T(2,128)(2,1)S(1)}, bf16[18,1,128]{2,1,0:T(2,128)(2,1)S(1)}, u32[]{:S(2)}, u32[]{:S(2)}) collective-permute-start(bf16[18,1,128]{2,1,0:T(2,128)(2,1)S(1)} %get-tuple-element.32), channel_id=1, source_target_pairs={{0,1},{1,2},{2,3},{4,5},{5,6},{6,7},{8,9},{9,10},{10,11},{12,13},{... | collective-permute-start | bytes 13832 | tf_op jit(solution)/shard_map/ppermute | solution.py:218
  146.3 1.3 collective-permute-start.3
  147.7 4.2 %collective-permute-done.3 = bf16[18,1,128]{2,1,0:T(2,128)(2,1)S(1)} collective-permute-done((bf16[18,1,128]{2,1,0:T(2,128)(2,1)S(1)}, bf16[18,1,128]{2,1,0:T(2,128)(2,1)S(1)}, u32[]{:S(2)}, u32[]{:S(2)}) %collective-permute-start.3) | collective-permute-done | bytes 4640 | tf_op jit(solution)/shard_map/ppermute | solution.py:219
  151.9 0.3 maximum_maximum_fusion
  152.2 0.4 fusion.12
  152.5 0.4 fusion.13
  152.9 0.8 fusion.5
  153.8 0.6 fusion.18
  154.3 0.6 convolution_add_fusion.3
  154.9 0.6 convolution_add_fusion.2
  155.6 0.3 multiply_convert_fusion
  155.9 2.0 collective-permute-start.4
  157.9 3.5 %collective-permute-start.5 = (bf16[1,128,128]{2,1,0:T(8,128)(2,1)S(1)}, bf16[1,128,128]{2,1,0:T(8,128)(2,1)S(1)}, u32[]{:S(2)}, u32[]{:S(2)}) collective-permute-start(bf16[1,128,128]{2,1,0:T(8,128)(2,1)S(1)} %get-tuple-element.37), channel_id=1, source_target_pairs={{4,0},{8,4},{12,8},{16,12},{20,16},{24,20},{28,24},{32,28},{36,32}... | collective-permute-start | bytes 98312 | tf_op jit(solution)/shard_map/ppermute | solution.py:219
  161.5 1.6 collective-permute-done.5
  163.1 3.4 %collective-permute-start.6 = (bf16[18,1,128]{2,1,0:T(2,128)(2,1)S(1)}, bf16[18,1,128]{2,1,0:T(2,128)(2,1)S(1)}, u32[]{:S(2)}, u32[]{:S(2)}) collective-permute-start(bf16[18,1,128]{2,1,0:T(2,128)(2,1)S(1)} %get-tuple-element.28), channel_id=1, source_target_pairs={{0,1},{1,2},{2,3},{4,5},{5,6},{6,7},{8,9},{9,10},{10,11},{12,13},{... | collective-permute-start | bytes 13832 | tf_op jit(solution)/shard_map/ppermute | solution.py:218
  166.5 1.3 collective-permute-start.7
  167.8 4.2 %collective-permute-done.7 = bf16[18,1,128]{2,1,0:T(2,128)(2,1)S(1)} collective-permute-done((bf16[18,1,128]{2,1,0:T(2,128)(2,1)S(1)}, bf16[18,1,128]{2,1,0:T(2,128)(2,1)S(1)}, u32[]{:S(2)}, u32[]{:S(2)}) %collective-permute-start.7) | collective-permute-done | bytes 4640 | tf_op jit(solution)/shard_map/ppermute | solution.py:219
  172.0 0.3 maximum_maximum_fusion.1
  172.3 0.4 fusion.10
  172.7 0.4 fusion.11
  173.1 0.8 fusion.1
  173.9 0.6 fusion.19
  174.5 0.6 convolution_add_fusion.1
  175.1 0.6 convolution_add_fusion
  175.7 0.4 copy-done
  176.1 1.4 add_convert_fusion
  177.8 0.5 broadcast_maximum_fusion.patch_ref
  178.3 0.5 convert_add_fusion.slot_ref
  178.8 31.0 %all-gather.2.cloned.1.call-done.tile_ref = bf16[64,128,128]{2,1,0:T(8,128)(2,1)} async-done(((bf16[16,128,128]{2,1,0:T(8,128)(2,1)}), bf16[64,128,128]{2,1,0:T(8,128)(2,1)}) %all-gather.2.cloned.1.call-update) | async-done | bytes 2097168 | tf_op jit(solution)/shard_map/all_gather | solution.py:327
  209.8 35.3 %read_and_return.1 = bf16[32,128,128]{2,1,0:T(8,128)(2,1)} custom-call(s32[64]{0:T(128)} %broadcast_maximum_fusion.patch_ref, s32[32]{0:T(128)} %convert_add_fusion.slot_ref, bf16[32,272,128]{2,1,0:T(8,128)(2,1)} %get-tuple-element.6.got_ref.meta_ref, bf16[64,128,128]{2,1,0:T(8,128)(2,1)} %all-gather.2.cloned.1.call-done.tile_ref, ...), custom_call_target="tpu_custom_call" | custom-call | tf_op jit(solution)/shard_map/read_and_return/pallas_call | solution.py:329
  245.1 2.3 copy.38
  (40 shorter events, 1.0 us)
Async XLA Ops:
  7.2 94.9 %reduce-scatter.5.cloned.1.call-start = ((), (), s32[]{:S(2)}) async-start(), calls=%async_computation.3 | async-start | bytes 20480 | tf_op jit(solution)/shard_map/reduce_scatter | solution.py:320
  75.8 58.3 %reduce-scatter.3.cloned.1.call-start = ((), (), s32[]{:S(2)}) async-start(), calls=%async_computation.2 | async-start | bytes 2621440 | tf_op jit(solution)/shard_map/reduce_scatter | solution.py:319
  79.3 54.7 %copy-start.4 = (f32[128]{0:T(128)S(1)}, f32[128]{0:T(128)}, u32[]{:S(2)}) copy-start(f32[128]{0:T(128)} %param.23) | copy-start | bytes 1540
  79.3 68.3 %copy-start.1 = (bf16[3,3,128,128]{3,2,1,0:T(8,128)(2,1)S(1)}, bf16[3,3,128,128]{3,2,1,0:T(8,128)(2,1)}, u32[]{:S(2)}) copy-start(bf16[3,3,128,128]{3,2,1,0:T(8,128)(2,1)} %param.24) | copy-start | bytes 884740
  79.4 130.4 %all-gather.2.cloned.1.call-start = ((), (), s32[]{:S(2)}) async-start(), calls=%async_computation.4 | async-start | bytes 2621440 | tf_op jit(solution)/shard_map/all_gather | solution.py:327
  135.7 5.6 %collective-permute-start = (bf16[1,128,128]{2,1,0:T(8,128)(2,1)S(1)}, bf16[1,128,128]{2,1,0:T(8,128)(2,1)S(1)}, u32[]{:S(2)}, u32[]{:S(2)}) collective-permute-start(bf16[1,128,128]{2,1,0:T(8,128)(2,1)S(1)} %get-tuple-element.43), channel_id=1, source_target_pairs={{0,4},{4,8},{8,12},{12,16},{16,20},{20,24},{24,28},{28,32},{32,36}... | collective-permute-start | bytes 98312 | tf_op jit(solution)/shard_map/ppermute | solution.py:218
  137.7 5.2 %collective-permute-start.1 = (bf16[1,128,128]{2,1,0:T(8,128)(2,1)S(1)}, bf16[1,128,128]{2,1,0:T(8,128)(2,1)S(1)}, u32[]{:S(2)}, u32[]{:S(2)}) collective-permute-start(bf16[1,128,128]{2,1,0:T(8,128)(2,1)S(1)} %get-tuple-element.42), channel_id=1, source_target_pairs={{4,0},{8,4},{12,8},{16,12},{20,16},{24,20},{28,24},{32,28},{36,32}... | collective-permute-start | bytes 98312 | tf_op jit(solution)/shard_map/ppermute | solution.py:219
  142.9 4.8 %collective-permute-start.2 = (bf16[18,1,128]{2,1,0:T(2,128)(2,1)S(1)}, bf16[18,1,128]{2,1,0:T(2,128)(2,1)S(1)}, u32[]{:S(2)}, u32[]{:S(2)}) collective-permute-start(bf16[18,1,128]{2,1,0:T(2,128)(2,1)S(1)} %get-tuple-element.32), channel_id=1, source_target_pairs={{0,1},{1,2},{2,3},{4,5},{5,6},{6,7},{8,9},{9,10},{10,11},{12,13},{... | collective-permute-start | bytes 13832 | tf_op jit(solution)/shard_map/ppermute | solution.py:218
  146.3 5.6 %collective-permute-start.3 = (bf16[18,1,128]{2,1,0:T(2,128)(2,1)S(1)}, bf16[18,1,128]{2,1,0:T(2,128)(2,1)S(1)}, u32[]{:S(2)}, u32[]{:S(2)}) collective-permute-start(bf16[18,1,128]{2,1,0:T(2,128)(2,1)S(1)} %get-tuple-element.33), channel_id=1, source_target_pairs={{1,0},{2,1},{3,2},{5,4},{6,5},{7,6},{9,8},{10,9},{11,10},{13,12},{... | collective-permute-start | bytes 13832 | tf_op jit(solution)/shard_map/ppermute | solution.py:219
  154.9 0.7 copy-start.5
  155.5 12.2 %copy-start.2 = (bf16[3,3,128,128]{3,2,1,0:T(8,128)(2,1)S(1)}, bf16[3,3,128,128]{3,2,1,0:T(8,128)(2,1)}, u32[]{:S(2)}) copy-start(bf16[3,3,128,128]{3,2,1,0:T(8,128)(2,1)} %param.26) | copy-start | bytes 884740
  155.9 5.6 %collective-permute-start.4 = (bf16[1,128,128]{2,1,0:T(8,128)(2,1)S(1)}, bf16[1,128,128]{2,1,0:T(8,128)(2,1)S(1)}, u32[]{:S(2)}, u32[]{:S(2)}) collective-permute-start(bf16[1,128,128]{2,1,0:T(8,128)(2,1)S(1)} %get-tuple-element.38), channel_id=1, source_target_pairs={{0,4},{4,8},{8,12},{12,16},{16,20},{20,24},{24,28},{28,32},{32,36}... | collective-permute-start | bytes 98312 | tf_op jit(solution)/shard_map/ppermute | solution.py:218
  157.9 5.1 %collective-permute-start.5 = (bf16[1,128,128]{2,1,0:T(8,128)(2,1)S(1)}, bf16[1,128,128]{2,1,0:T(8,128)(2,1)S(1)}, u32[]{:S(2)}, u32[]{:S(2)}) collective-permute-start(bf16[1,128,128]{2,1,0:T(8,128)(2,1)S(1)} %get-tuple-element.37), channel_id=1, source_target_pairs={{4,0},{8,4},{12,8},{16,12},{20,16},{24,20},{28,24},{32,28},{36,32}... | collective-permute-start | bytes 98312 | tf_op jit(solution)/shard_map/ppermute | solution.py:219
  163.1 4.8 %collective-permute-start.6 = (bf16[18,1,128]{2,1,0:T(2,128)(2,1)S(1)}, bf16[18,1,128]{2,1,0:T(2,128)(2,1)S(1)}, u32[]{:S(2)}, u32[]{:S(2)}) collective-permute-start(bf16[18,1,128]{2,1,0:T(2,128)(2,1)S(1)} %get-tuple-element.28), channel_id=1, source_target_pairs={{0,1},{1,2},{2,3},{4,5},{5,6},{6,7},{8,9},{9,10},{10,11},{12,13},{... | collective-permute-start | bytes 13832 | tf_op jit(solution)/shard_map/ppermute | solution.py:218
  166.5 5.6 %collective-permute-start.7 = (bf16[18,1,128]{2,1,0:T(2,128)(2,1)S(1)}, bf16[18,1,128]{2,1,0:T(2,128)(2,1)S(1)}, u32[]{:S(2)}, u32[]{:S(2)}) collective-permute-start(bf16[18,1,128]{2,1,0:T(2,128)(2,1)S(1)} %get-tuple-element.29), channel_id=1, source_target_pairs={{1,0},{2,1},{3,2},{5,4},{6,5},{7,6},{9,8},{10,9},{11,10},{13,12},{... | collective-permute-start | bytes 13832 | tf_op jit(solution)/shard_map/ppermute | solution.py:219
  175.1 1.0 copy-start
  175.1 1.0 copy-start.6
  175.7 1.9 copy-start.7
  175.7 2.0 copy-start.3
Sparse Core Ops, SparseCore 0:
  75.9 26.1 reduce-scatter.4
  104.5 29.5 reduce-scatter.2
  177.7 32.0 all-gather.1

commit v2 on v1

--- a/solution.py
+++ b/solution.py
@@ -15,6 +15,9 @@
 BLK = 128
 C = 128
 MOST = 2
+CELLS = PH * PW
+PATCHES = SR // PH * (TC // PW)
+DENS = 2 * PATCHES
 PAIR = MOST * BLK + 16
 MESH = pl.DeviceIdType.MESH
 VMEM = pltpu.VMEM
@@ -120,7 +123,7 @@
     lax.fori_loop(1, tiles, finish, 0)
 
 
-def spread_kernel(tiles, patches, patch_ref, got_ref, spread_ref, density_ref, acc, density_acc):
+def spread_kernel(tiles, orbits, group, patch_ref, got_ref, part_ref, acc, density_acc):
     step = pl.program_id(0)
 
     @pl.when(step == 0)
@@ -128,35 +131,207 @@
         acc[...] = jnp.zeros_like(acc)
         density_acc[...] = jnp.zeros_like(density_acc)
 
-    metas = got_ref[0, MOST * BLK :, :].astype(jnp.float32)
     ones = jnp.ones((8, BLK), jnp.bfloat16)
-    for j in range(MOST):
-        patch = patch_ref[step * MOST + j]
-
-        @pl.when(patch >= 0)
-        def _():
+    found = []
+    for g in range(group):
+        metas = got_ref[g, MOST * BLK :, :].astype(jnp.float32)
+        for j in range(MOST):
             matrix = window_weights(metas[8 * j : 8 * j + 8])
-            acc[patch] += jnp.dot(matrix, got_ref[0, j * BLK : (j + 1) * BLK, :], preferred_element_type=jnp.float32)
+            spread = jnp.dot(matrix, got_ref[g, j * BLK : (j + 1) * BLK, :], preferred_element_type=jnp.float32)
             sums = lax.dot_general(ones, matrix, (((1,), (1,)), ((), ())), preferred_element_type=jnp.float32)
-            density_acc[pl.ds(patch, 1), :] += sums[0:1]
-
-    @pl.when(step == tiles - 1)
+            found.append((patch_ref[(step * group + g) * MOST + j], spread, sums[0:1]))
+    for patch, spread, sums in found:
+        acc[patch] += spread
+        density_acc[pl.ds(patch, 1), :] += sums
+
+    @pl.when(step == tiles // group - 1)
     def _():
-        spread_ref[...] = acc[...].astype(jnp.bfloat16)
-        density_ref[...] = density_acc[...].astype(jnp.bfloat16)
-
-
-def read_kernel(
-    tiles, cols, blocks, patch_ref, slot_ref, meta_ref, tile_ref, features_ref,
-    out_ref, values_ref, send, got, send_sem, recv_sem,
+        own = PATCHES
+        for z in range(orbits):
+            part_ref[z, : own * CELLS, :] = acc[z * own : (z + 1) * own].reshape(own * CELLS, C).astype(jnp.bfloat16)
+            sums = density_acc[z * own : (z + 1) * own, :]
+            rows = jnp.concatenate([sums[:, :C], sums[:, C:]], axis=0)
+            part_ref[z, own * CELLS :, :] = rows.astype(jnp.bfloat16)
+
+
+def grid_kernel(
+    rows, cols, blocks, patch_ref, slot_ref, part_ref, meta_ref, features_ref, dw_ref, w1_ref, b1_ref, w2_ref, b2_ref,
+    out_ref, grid_ref,
+    relay_in, relay_out, part_in, tile, wide, first, col_out, row_in, col_in, mine, values, send, got,
+    ring_send, ring_recv, gather_send, gather_recv, edge_send, edge_recv, send_sem, recv_sem,
 ):
-    me = lax.axis_index("rows") * cols + lax.axis_index("cols")
-    plane_barrier(me, tiles, cols)
-    across = TC // PW
-    for p in range(values_ref.shape[0]):
-        top, left = p // across * PH, p % across * PW
-        values_ref[p] = tile_ref[top : top + PH, left : left + PW, :].reshape(PH * PW, C)
-    ones = jnp.ones((PH * PW, C), jnp.bfloat16)
+    z, r, c = lax.axis_index("orbits"), lax.axis_index("rows"), lax.axis_index("cols")
+    orbits = 4
+    tiles = rows * cols
+    stripes = orbits * rows
+    me = r * cols + c
+    stripe = z * rows + r
+    after, before = (z + 1) % orbits, (z + orbits - 1) % orbits
+    across = (z + 2) % orbits
+    half = PATCHES * CELLS // 2
+
+    def edge_device(up, side):
+        other = (stripe + stripes + up) % stripes
+        return (other // rows, other % rows, (c + cols + side) % cols)
+
+    edges = ((-1, 0), (1, 0), (-1, -1), (0, -1), (1, -1), (-1, 1), (0, 1), (1, 1))
+    barrier = pltpu.get_barrier_semaphore()
+
+    def greet(k, carry):
+        pl.semaphore_signal(barrier, inc=1, device_id=plane_device((me + k) % tiles, cols), device_id_type=MESH)
+        return carry
+
+    lax.fori_loop(1, tiles, greet, 0)
+    for other in (after, before):
+        pl.semaphore_signal(barrier, inc=1, device_id=(other, r, c), device_id_type=MESH)
+    for up, side in edges:
+        pl.semaphore_signal(barrier, inc=1, device_id=edge_device(up, side), device_id_type=MESH)
+    pl.semaphore_wait(barrier, tiles - 1 + 2 + len(edges))
+
+    sides = ((0, after, pl.ds(0, half), pl.ds(half, half + DENS)), (1, before, pl.ds(half, half + DENS), pl.ds(0, half)))
+
+    def ring_copy(src, dst, way, step, other):
+        return pltpu.make_async_remote_copy(
+            src_ref=src, dst_ref=dst, send_sem=ring_send.at[way, step], recv_sem=ring_recv.at[way, step],
+            device_id=(other, r, c), device_id_type=MESH,
+        )
+
+    ring = []
+    for way, other, passed, direct in sides:
+        relay = ring_copy(part_ref.at[across, passed], relay_in.at[passed], way, 0, other)
+        straight = ring_copy(part_ref.at[other, direct], part_in.at[way, direct], way, 1, other)
+        summed = ring_copy(relay_out.at[passed], part_in.at[way, passed], way, 2, other)
+        relay.start()
+        straight.start()
+        ring.append((relay, straight, summed))
+    for way, other, passed, direct in sides:
+        relay, straight, summed = ring[way]
+        relay.wait_recv()
+        total = part_ref[other, passed].astype(jnp.float32) + relay_in[passed].astype(jnp.float32)
+        relay_out[passed] = total.astype(jnp.bfloat16)
+        summed.start()
+    for relay, straight, summed in ring:
+        straight.wait_recv()
+    for relay, straight, summed in ring:
+        summed.wait_recv()
+
+    tail = pl.ds(PATCHES * CELLS, DENS)
+    parts = jnp.concatenate([part_ref[z, tail], part_in[0, tail], part_in[1, tail]], axis=0)
+    picked = lax.broadcasted_iota(jnp.int32, (3 * DENS, DENS * C), 0) % DENS == lax.broadcasted_iota(jnp.int32, (3 * DENS, DENS * C), 1) // C
+    density_all = lax.dot_general(
+        parts, picked.astype(jnp.bfloat16), (((0,), (0,)), ((), ())), preferred_element_type=jnp.float32
+    )
+    weight = dw_ref[...]
+    wide_patches = TC // PW
+    for p in range(PATCHES):
+        for h in range(2):
+            k = h * PATCHES + p
+            density = density_all[:, k * C : (k + 1) * C]
+            cells = pl.ds(p * CELLS + h * C, C)
+            total = part_ref[z, cells].astype(jnp.float32) + part_in[0, cells].astype(jnp.float32) + part_in[1, cells].astype(jnp.float32)
+            value = total / jnp.maximum(density, 1.0) + weight * (density / (1.0 + density))
+            top, left = p // wide_patches * PH + h * (PH // 2), p % wide_patches * PW
+            tile[top : top + PH // 2, left : left + PW, :] = value.astype(jnp.bfloat16).reshape(PH // 2, PW, C)
+
+    row_id = lax.broadcasted_iota(jnp.int32, (TC, C), 0)
+
+    def exchange(source, turn):
+        for i in range(SR):
+            col_out[turn, 0, i : i + 1, :] = source[i, 0:1, :]
+            col_out[turn, 1, i : i + 1, :] = source[i, TC - 1 : TC, :]
+        copies = []
+        for e, (up, side) in enumerate(edges):
+            if side == 0:
+                src, dst = source.at[0 if up < 0 else SR - 1], row_in.at[turn, e]
+            else:
+                src, dst = col_out.at[turn, 0 if side < 0 else 1], col_in.at[turn, e - 2]
+            copies.append(pltpu.make_async_remote_copy(
+                src_ref=src, dst_ref=dst, send_sem=edge_send.at[turn, e], recv_sem=edge_recv.at[turn, e],
+                device_id=edge_device(up, side), device_id_type=MESH,
+            ))
+        for copy in copies:
+            copy.start()
+
+        def shifts(row, centre):
+            centre = centre.astype(jnp.float32)
+            wide[row, :, 0:C] = pltpu.roll(centre, 1, 0).astype(jnp.bfloat16)
+            wide[row, :, C : 2 * C] = centre.astype(jnp.bfloat16)
+            wide[row, :, 2 * C :] = pltpu.roll(centre, TC - 1, 0).astype(jnp.bfloat16)
+
+        for i in range(SR):
+            shifts(i + 1, source[i])
+        for copy in copies:
+            copy.wait_recv()
+        from_above, from_below = row_in[turn, 1], row_in[turn, 0]
+        shifts(0, jnp.where(stripe > 0, from_above.astype(jnp.float32), 0.0))
+        shifts(SR + 1, jnp.where(stripe < stripes - 1, from_below.astype(jnp.float32), 0.0))
+        left_open, right_open = c > 0, c < cols - 1
+        for first_edge, lanes, at, open_ in ((3, slice(0, C), 0, left_open), (0, slice(2 * C, 3 * C), TC - 1, right_open)):
+            above = col_in[turn, first_edge + 2, SR - 1 : SR, :].astype(jnp.float32)
+            level = col_in[turn, first_edge + 1].astype(jnp.float32)
+            below = col_in[turn, first_edge, 0:1, :].astype(jnp.float32)
+            above = jnp.where(open_ & (stripe > 0), above, 0.0)
+            level = jnp.where(open_, level, 0.0)
+            below = jnp.where(open_ & (stripe < stripes - 1), below, 0.0)
+            wide[0, at : at + 1, lanes] = above.astype(jnp.bfloat16)
+            wide[SR + 1, at : at + 1, lanes] = below.astype(jnp.bfloat16)
+            for i in range(SR):
+                wide[i + 1, at : at + 1, lanes] = level[i : i + 1].astype(jnp.bfloat16)
+        return copies
+
+    block_rows = 4
+
+    def convolved(i, w_ref, b_ref):
+        total = None
+        for a in range(3):
+            x = wide[pl.ds(i + a, block_rows)].reshape(block_rows * TC, 3 * C)
+            term = jnp.dot(x, w_ref[a], preferred_element_type=jnp.float32)
+            total = term if total is None else total + term
+        return total + b_ref[...]
+
+    edge_copies = exchange(tile, 0)
+    for i in range(0, SR, block_rows):
+        v = convolved(i, w1_ref, b1_ref)
+        v = v / (1.0 + jnp.exp(-v))
+        first[i : i + block_rows] = v.astype(jnp.bfloat16).reshape(block_rows, TC, C)
+    edge_copies += exchange(first, 1)
+
+    count = PATCHES // 2
+
+    def half_of(owner, h):
+        return values.at[pl.ds(owner * PATCHES + h * count, count)]
+
+    def gather_copy(owner, h, way, step, other, src):
+        return pltpu.make_async_remote_copy(
+            src_ref=src, dst_ref=half_of(owner, h), send_sem=gather_send.at[way, step], recv_sem=gather_recv.at[way, step],
+            device_id=(other, r, c), device_id_type=MESH,
+        )
+
+    gathers = []
+    for h in range(2):
+        for i in range(h * PH, (h + 1) * PH, block_rows):
+            v = convolved(i, w2_ref, b2_ref).reshape(block_rows, TC, C)
+            v = (tile[i : i + block_rows].astype(jnp.float32) + v).astype(jnp.bfloat16)
+            grid_ref[i : i + block_rows] = v
+            for q in range(wide_patches):
+                cells = pl.ds((i - h * PH) * PW, block_rows * PW)
+                mine[h * count + q, cells, :] = v[:, q * PW : (q + 1) * PW, :].reshape(block_rows * PW, C)
+        for way, other in ((0, after), (1, before)):
+            copy = gather_copy(z, h, way, h, other, mine.at[pl.ds(h * count, count)])
+            copy.start()
+            gathers.append(copy)
+    values[pl.ds(z * PATCHES, PATCHES)] = mine[...]
+    for way, other, owner in ((0, after, before), (1, before, after)):
+        gather_copy(owner, way, way, way, other, half_of(owner, way)).wait_recv()
+        copy = gather_copy(owner, way, way, 2, other, half_of(owner, way))
+        copy.start()
+        gathers.append(copy)
+    for way, other, owner in ((0, after, before), (1, before, after)):
+        gather_copy(owner, 1 - way, way, 1 - way, other, half_of(owner, 1 - way)).wait_recv()
+    for way, other in ((0, after), (1, before)):
+        gather_copy(across, way, way, 2, other, half_of(across, way)).wait_recv()
+
+    ones = jnp.ones((CELLS, C), jnp.bfloat16)
 
     def pair(t):
         return pl.ds(t * MOST, MOST)
@@ -176,11 +351,11 @@
     def read(s, target):
         metas = meta_ref[s].astype(jnp.float32)
         for j in range(MOST):
-            rows = metas[8 * j : 8 * j + 8]
-            row_id = lax.broadcasted_iota(jnp.int32, (8, BLK), 0)
-            rows = jnp.where((row_id == 2) & (rows < 0.0), 0.0, rows)
-            matrix = window_weights(rows)
-            both = jnp.concatenate([values_ref[patch_ref[s * MOST + j]], ones], axis=1)
+            meta = metas[8 * j : 8 * j + 8]
+            meta_id = lax.broadcasted_iota(jnp.int32, (8, BLK), 0)
+            meta = jnp.where((meta_id == 2) & (meta < 0.0), 0.0, meta)
+            matrix = window_weights(meta)
+            both = jnp.concatenate([values[patch_ref[s * MOST + j]], ones], axis=1)
             summed = lax.dot_general(matrix, both, (((0,), (0,)), ((), ())), preferred_element_type=jnp.float32)
             target[s * MOST + j] = (summed[:, :C] / summed[:, C:]).astype(jnp.bfloat16)
 
@@ -206,46 +381,11 @@
         return carry
 
     lax.fori_loop(0, blocks, combine, 0)
-
-
-def extended(x, sides, width):
-    for axis, dim in sides:
-        size, length = (lax.axis_size(axis), x.shape[dim])
-        up = [(i, (i + 1) % size) for i in range(size - 1)]
-        down = [(j, i) for i, j in up]
-        last = lax.slice_in_dim(x, length - width, length, axis=dim)
-        initial = lax.slice_in_dim(x, 0, width, axis=dim)
-        before = lax.ppermute(last, axis, up)
-        after = lax.ppermute(initial, axis, down)
-        x = jnp.concatenate([before, x, after], axis=dim)
-    return x
-
-
-def convolve(padded, weight, bias_vec):
-    height = padded.shape[-3] - 2
-    breadth = padded.shape[-2] - 2
-    channels = padded.shape[-1]
-    summed = None
-    for row_shift in range(3):
-        rows_part = padded[row_shift : row_shift + height]
-        stacked = jnp.concatenate([rows_part[:, s : s + breadth, :] for s in range(3)], axis=-1)
-        term = jnp.dot(
-            stacked.reshape(-1, 3 * channels), weight[row_shift].reshape(3 * channels, channels),
-            preferred_element_type=jnp.float32,
-        )
-        summed = term if summed is None else summed + term
-    return summed.reshape((height, breadth, channels)) + bias_vec
-
-
-def patches_to_tile(patches, tile_height, tile_width):
-    trailing = patches.shape[2:]
-    shaped = patches.reshape((tile_height // PH, tile_width // PW, PH, PW) + trailing)
-    axes_order = (0, 2, 1, 3) + tuple(range(4, 4 + len(trailing)))
-    return shaped.transpose(axes_order).reshape((tile_height, tile_width) + trailing)
-
-
-def plain_edges(stripe):
-    return extended(stripe, ((("orbits", "rows"), 0), ("cols", 1)), 1)
+    for copies in ring:
+        for copy in copies:
+            copy.wait_send()
+    for copy in gathers + edge_copies:
+        copy.wait_send()
 
 
 def local(
@@ -294,54 +434,60 @@
     )(jnp.maximum(block_of_slot, 0), patch_at, obs_feat.reshape(blocks, BLK, C), obs_offset, obs_cells, w_embed, b_embed[None, :], w_proj, b_proj[None, :])
 
     got_patch = jnp.stack([got[:, MOST * BLK + 4, 0], got[:, MOST * BLK + 12, 0]], axis=1).astype(jnp.int32).reshape(slots)
-
-    spread, density = pl.pallas_call(
-        functools.partial(spread_kernel, tiles, patches),
+    got_patch = jnp.maximum(got_patch, 0)
+
+    group = min(4, tiles)
+    rows_out = PATCHES * CELLS + DENS
+    part = pl.pallas_call(
+        functools.partial(spread_kernel, tiles, orbits, group),
         grid_spec=pltpu.PrefetchScalarGridSpec(
             num_scalar_prefetch=1,
-            grid=(tiles,),
-            in_specs=[pl.BlockSpec((1, PAIR, C), lambda i, p: (i, 0, 0))],
-            out_specs=(
-                pl.BlockSpec((patches, PH * PW, C), lambda i, p: (0, 0, 0)),
-                pl.BlockSpec((patches, PH * PW), lambda i, p: (0, 0)),
-            ),
-            scratch_shapes=[VMEM((patches, PH * PW, C), jnp.float32), VMEM((patches, PH * PW), jnp.float32)],
+            grid=(tiles // group,),
+            in_specs=[pl.BlockSpec((group, PAIR, C), lambda i, p: (i, 0, 0))],
+            out_specs=pl.BlockSpec((orbits, rows_out, C), lambda i, p: (0, 0, 0)),
+            scratch_shapes=[VMEM((patches, CELLS, C), jnp.float32), VMEM((patches, CELLS), jnp.float32)],
         ),
-        out_shape=(
-            jax.ShapeDtypeStruct((patches, PH * PW, C), jnp.bfloat16),
-            jax.ShapeDtypeStruct((patches, PH * PW), jnp.bfloat16),
-        ),
+        out_shape=jax.ShapeDtypeStruct((orbits, rows_out, C), jnp.bfloat16),
         name="spread",
     )(got_patch, got)
 
-    spread_tile = patches_to_tile(spread, tile_height, TC)
-    density_tile = patches_to_tile(density, tile_height, TC)
-    spread_part = lax.psum_scatter(spread_tile, "orbits", scatter_dimension=0, tiled=True).astype(jnp.float32)
-    density_part = lax.psum_scatter(density_tile, "orbits", scatter_dimension=0, tiled=True).astype(jnp.float32)
-    grid_in = (
-        spread_part / jnp.maximum(density_part, 1.0)[..., None]
-        + density_weight * (density_part / (1.0 + density_part))[..., None]
-    ).astype(jnp.bfloat16)
-    first = jax.nn.silu(convolve(plain_edges(grid_in), w_first, b_first)).astype(jnp.bfloat16)
-    grid_out = (grid_in.astype(jnp.float32) + convolve(plain_edges(first), w_second, b_second)).astype(jnp.bfloat16)
-    full_out = lax.all_gather(grid_out, "orbits", axis=0, tiled=True)
-
-    obs_out = pl.pallas_call(
-        functools.partial(read_kernel, tiles, cols, blocks),
+    half = PATCHES * CELLS // 2
+    bf = jnp.bfloat16
+    obs_out, grid_out = pl.pallas_call(
+        functools.partial(grid_kernel, tiles // cols, cols, blocks),
         grid=(1,),
-        out_shape=jax.ShapeDtypeStruct((blocks, BLK, C), jnp.bfloat16),
-        in_specs=[sm, sm, pl.BlockSpec((tiles, 16, C), lambda i: (0, MOST * BLK // 16, 0)), vm, vm],
-        out_specs=vm,
+        out_shape=(jax.ShapeDtypeStruct((blocks, BLK, C), bf), jax.ShapeDtypeStruct((SR, TC, C), bf)),
+        in_specs=[sm, sm, vm, pl.BlockSpec((tiles, 16, C), lambda i: (0, MOST * BLK // 16, 0)), vm, vm, vm, vm, vm, vm],
+        out_specs=(vm, vm),
         scratch_shapes=[
-            VMEM((patches, PH * PW, C), jnp.bfloat16),
-            VMEM((slots, BLK, C), jnp.bfloat16),
-            VMEM((slots, BLK, C), jnp.bfloat16),
+            VMEM((rows_out, C), bf),
+            VMEM((rows_out, C), bf),
+            VMEM((2, rows_out, C), bf),
+            VMEM((SR, TC, C), bf),
+            VMEM((SR + 2, TC, 3 * C), bf),
+            VMEM((SR, TC, C), bf),
+            VMEM((2, 2, SR, C), bf),
+            VMEM((2, 2, TC, C), bf),
+            VMEM((2, 6, SR, C), bf),
+            VMEM((PATCHES, CELLS, C), bf),
+            VMEM((patches, CELLS, C), bf),
+            VMEM((slots, BLK, C), bf),
+            VMEM((slots, BLK, C), bf),
+            pltpu.SemaphoreType.DMA((2, 3)),
+            pltpu.SemaphoreType.DMA((2, 3)),
+            pltpu.SemaphoreType.DMA((2, 3)),
+            pltpu.SemaphoreType.DMA((2, 3)),
+            pltpu.SemaphoreType.DMA((2, 8)),
+            pltpu.SemaphoreType.DMA((2, 8)),
             pltpu.SemaphoreType.DMA((tiles,)),
             pltpu.SemaphoreType.DMA((tiles,)),
         ],
-        compiler_params=pltpu.CompilerParams(collective_id=1, has_side_effects=True),
-        name="read_and_return",
-    )(jnp.maximum(got_patch, 0), slot_of, got, full_out, features)
+        compiler_params=pltpu.CompilerParams(collective_id=1, has_side_effects=True, vmem_limit_bytes=60000000),
+        name="grid_and_read",
+    )(
+        got_patch, slot_of, part, got, features, density_weight[None, :],
+        w_first.reshape(3, 3 * C, C), b_first[None, :], w_second.reshape(3, 3 * C, C), b_second[None, :],
+    )
     return (obs_out.reshape(obs_feat.shape), grid_out)
 
 

time: 258 us -> 155 us (0.60)
  the two profiles are of different devices: /device:TPU:2 before, /device:TPU:25 now
where the time goes in v2:
time: 155 us
  Pallas kernels  145 us (94%)
  local copies, waits for them, and re-layouts  5.22 us (3%)
  other arithmetic  4.19 us (3%)
    pallas_call x1, Pallas kernels, local(): pl.pallas_call(functools.partial(grid_kernel, tiles // cols, cols, blocks...  93.8 us
    pallas_call x1, Pallas kernels, local(): pl.pallas_call(functools.partial(scatter_kernel, tiles, cols, blocks), gr...  42.3 us
    pallas_call x1, Pallas kernels, local(): pl.pallas_call(functools.partial(spread_kernel, tiles, orbits, group), gr...  8.46 us
    unnamed x4, local copies, waits for them, and re-layouts  3.12 us

profile of v2, /device:TPU:25, one launch (start us, length us, event | category | flops | bytes accessed | tf_op | source)
XLA Modules:
  0.0 154.7 jit_solution(1115897730730977832)
XLA Ops:
  0.6 0.7 broadcast_add_fusion.1
  1.3 0.9 fusion.1
  2.2 1.2 convert_add_fusion.slot_ref
  3.4 0.8 select_reduce_fusion.2
  4.2 0.1 copy.20
  4.3 0.1 reshape.57
  4.4 0.1 select_reduce_fusion
  4.5 0.5 broadcast_add_fusion
  5.0 42.3 %embed_and_send.1 = (bf16[32,128,128]{2,1,0:T(8,128)(2,1)}, bf16[32,272,128]{2,1,0:T(8,128)(2,1)}) custom-call(s32[64]{0:T(128)} %get-tuple-element.17.block_ref, s32[64]{0:T(128)} %get-tuple-element.16.patch_ref, bf16[32,128,128]{2,1,0:T(8,128)(2,1)} %bitcast.17, bf16[2,4096]{1,0:T(2,128)(2,1)} %off_ref.1, s32[16,4096]{1,0:T(8,128)} %cells_ref.1, ...), custom_call_target="tpu_custom_call" | custom-call | tf_op jit(solution)/shard_map/embed_and_send/pallas_call | solution.py:416
  47.4 1.2 slice_reduce_fusion.1
  48.6 0.1 copy.21
  48.7 0.6 max.10.patch_ref
  49.3 8.5 %spread.1.part_ref = bf16[4,2064,128]{2,1,0:T(8,128)(2,1)} custom-call(s32[64]{0:T(128)} %max.10.patch_ref, bf16[32,272,128]{2,1,0:T(8,128)(2,1)} %get-tuple-element.6.got_ref.meta_ref), custom_call_target="tpu_custom_call" | custom-call | tf_op jit(solution)/shard_map/spread/pallas_call | solution.py:441
  57.7 93.8 %grid_and_read.1 = (bf16[32,128,128]{2,1,0:T(8,128)(2,1)}, bf16[16,128,128]{2,1,0:T(8,128)(2,1)}) custom-call(s32[64]{0:T(128)} %max.10.patch_ref, s32[32]{0:T(128)} %convert_add_fusion.slot_ref, bf16[4,2064,128]{2,1,0:T(8,128)(2,1)} %spread.1.part_ref, bf16[32,272,128]{2,1,0:T(8,128)(2,1)} %get-tuple-element.6.got_ref.meta_ref, ...), custom_call_target="tpu_custom_call" | custom-call | tf_op jit(solution)/shard_map/grid_and_read/pallas_call | solution.py:456
  151.5 0.0 copy-start
  151.5 2.3 %copy.24 = bf16[4096,128]{1,0:T(8,128)(2,1)} copy(bf16[4096,128]{1,0:T(8,128)(2,1)} %bitcast.18) | data formatting | bytes 2097152
  153.9 0.0 copy-done
  153.9 0.8 copy.25
  (3 shorter events, 0.0 us)
Async XLA Ops:
  151.5 2.3 %copy-start = (bf16[16,128,128]{2,1,0:T(8,128)(2,1)S(1)}, bf16[16,128,128]{2,1,0:T(8,128)(2,1)}, u32[]{:S(2)}) copy-start(bf16[16,128,128]{2,1,0:T(8,128)(2,1)} %get-tuple-element.21) | copy-start | bytes 1572868

commit v3 on v1

v3 whole, which is shorter than its diff:
```python
import functools

import jax
import jax.numpy as jnp
from jax import lax
from jax.experimental import pallas as pl
from jax.experimental.pallas import tpu as pltpu
from jax.sharding import PartitionSpec as P

PH = 8
PW = 32
SR = 16
TC = 128
BLK = 128
C = 128
HALF = C // 2
MOST = 2
CELLS = PH * PW
FOLD = CELLS // 2
WIDE = TC // PW
PATCHES = SR // PH * WIDE
DENS = 2 * PATCHES
META = 16
ORBITS = 4
MESH = pl.DeviceIdType.MESH
VMEM = pltpu.VMEM
SMEM = pltpu.SMEM
BF = jnp.bfloat16
F32 = jnp.float32


def table_kernel(blocks, slots, tile_ref, patch_ref, block_at, patch_at, rank_of, count):
    def clear(s, carry):
        block_at[s] = 0
        patch_at[s] = -1
        return carry

    def empty(t, carry):
        count[t] = 0
        return carry

    lax.fori_loop(0, slots, clear, 0)
    lax.fori_loop(0, slots // MOST, empty, 0)

    def place(b, carry):
        t = tile_ref[b]
        rank = count[t]
        count[t] = rank + 1
        rank_of[b] = rank
        block_at[t * MOST + rank] = b
        patch_at[t * MOST + rank] = patch_ref[b]
        return carry

    lax.fori_loop(0, blocks, place, 0)


def window_weights(meta_rows):
    off_r, off_c = meta_rows[0:1], meta_rows[1:2]
    anchor_r, anchor_c = meta_rows[2:3], meta_rows[3:4]
    tap_r = lax.broadcasted_iota(jnp.int32, (PH, BLK), 0).astype(F32) - anchor_r
    tap_c = lax.broadcasted_iota(jnp.int32, (PW, BLK), 0).astype(F32) - anchor_c
    delta_r = tap_r - 1.5 - off_r
    delta_c = tap_c - 1.5 - off_c
    weight_r = jnp.where((tap_r >= 0.0) & (tap_r < 4.0), jnp.exp(delta_r * delta_r * -0.5), 0.0)
    weight_c = jnp.where((tap_c >= 0.0) & (tap_c < 4.0), jnp.exp(delta_c * delta_c * -0.5), 0.0)
    return jnp.concatenate([(weight_r[r : r + 1] * weight_c).astype(BF) for r in range(PH)], axis=0)


def swapped(x):
    return pltpu.roll(x.astype(F32), HALF, 1)


def main_kernel(
    rows, cols, blocks,
    block_at, patch_at, tile_of, rank_of,
    feat_ref, off_ref, cells_ref, we_ref, be_ref, wp_ref, bp_ref, dw_ref, w1_ref, b1_ref, w2_ref, b2_ref,
    out_ref, grid_ref,
    features, swapped_features, block_meta, send0, send1, got0, got1, matrices, patch_rows,
    sums0, sums1, density_sums, links, links_smem, density_rows, part0, part1, density_part, relay_in, relay_out, part_in,
    packed, tile, wide, first, col_out, row_in, col_in, mine, values0, values1, values_swapped, back_out, back_in,
    out_send, out_recv, ring_send, ring_recv, edge_send, edge_recv, gather_send, gather_recv, back_send, back_recv, link_sem,
):
    z, r, c = lax.axis_index("orbits"), lax.axis_index("rows"), lax.axis_index("cols")
    tiles = rows * cols
    slots = tiles * MOST
    stripes = ORBITS * rows
    stripe = z * rows + r
    after, before = (z + 1) % ORBITS, (z + ORBITS - 1) % ORBITS
    across = (z + 2) % ORBITS

    def offset_of(j):
        return (j - 1 + tiles // 2) % (tiles - 1) + 1

    def target(j):
        k = offset_of(j)
        return (r + k // cols) % rows, (c + k % cols) % cols

    def source(j):
        k = offset_of(j)
        return (r + rows - k // cols) % rows, (c + cols - k % cols) % cols

    def edge_device(up, side):
        other = (stripe + stripes + up) % stripes
        return (other // rows, other % rows, (c + cols + side) % cols)

    edges = ((-1, 0), (1, 0), (-1, -1), (0, -1), (1, -1), (-1, 1), (0, 1), (1, 1))
    barrier = pltpu.get_barrier_semaphore()

    def greet(j, carry):
        pl.semaphore_signal(barrier, inc=1, device_id=(z, *target(j)), device_id_type=MESH)
        return carry

    lax.fori_loop(1, tiles, greet, 0)
    for other in (after, before):
        pl.semaphore_signal(barrier, inc=1, device_id=(other, r, c), device_id_type=MESH)
    for up, side in edges:
        pl.semaphore_signal(barrier, inc=1, device_id=edge_device(up, side), device_id_type=MESH)

    group = min(4, blocks)
    proj = jnp.concatenate([wp_ref[...], swapped(wp_ref[...]).astype(BF)], axis=1)
    proj_bias = jnp.concatenate([bp_ref[...], jnp.concatenate([bp_ref[:, HALF:], bp_ref[:, :HALF]], axis=1)], axis=1)

    def embed(i, carry):
        at = pl.ds(i * group, group)
        x = feat_ref[at].reshape(group * BLK, C)
        v = jnp.dot(x, we_ref[...], preferred_element_type=F32) + be_ref[...]
        hidden = (v / (1.0 + jnp.exp(-v))).astype(BF)
        both = (jnp.dot(hidden, proj, preferred_element_type=F32) + proj_bias).astype(BF)
        features[at] = both[:, :C].reshape(group, BLK, C)
        swapped_features[at] = both[:, C:].reshape(group, BLK, C)
        return carry

    lax.fori_loop(0, blocks // group, embed, 0)
    row_id = lax.broadcasted_iota(jnp.int32, (8, BLK), 0)
    for b in range(blocks):
        lanes = slice(b * BLK, (b + 1) * BLK)
        off = off_ref[:, lanes].astype(F32)
        cell = cells_ref[0:1, lanes]
        meta = jnp.where(row_id == 0, off[0:1], 0.0)
        meta = jnp.where(row_id == 1, off[1:2], meta)
        meta = jnp.where(row_id == 2, (cell >> 5).astype(F32), meta)
        block_meta[b] = jnp.where(row_id == 3, (cell & 31).astype(F32), meta)

    low_lanes = lax.broadcasted_iota(jnp.int32, (BLK, C), 1) < HALF

    def pack(t, dst0, dst1, j):
        at = [block_at[t * MOST + i] for i in range(MOST)]
        dst0[j, :BLK, :] = jnp.where(low_lanes, features[at[0]], swapped_features[at[1]])
        dst1[j] = jnp.where(low_lanes, swapped_features[at[0]], features[at[1]])
        metas = []
        for i in range(MOST):
            patch = jnp.full((8, BLK), patch_at[t * MOST + i].astype(F32))
            meta = jnp.where((row_id == 2) & (patch < 0.0), -100.0, block_meta[at[i]])
            metas.append(jnp.where(row_id == 4, patch, meta))
        dst0[j, BLK:, :] = jnp.concatenate(metas, axis=0).astype(BF)

    sends, gots = (send0, send1), (got0, got1)

    def out_copy(q, j):
        return pltpu.make_async_remote_copy(
            src_ref=sends[q].at[j], dst_ref=gots[q].at[j], send_sem=out_send.at[q, j], recv_sem=out_recv.at[q, j],
            device_id=(z, *target(j)), device_id_type=MESH,
        )

    pl.semaphore_wait(barrier, tiles - 1 + 2 + len(edges))

    def start_first(j, carry):
        tr, tc = target(j)
        pack(tr * cols + tc, send0, send1, j)
        out_copy(0, j).start()
        return carry

    def start_second(j, carry):
        out_copy(1, j).start()
        return carry

    lax.fori_loop(1, tiles, start_first, 0)
    lax.fori_loop(1, tiles, start_second, 0)
    pack(r * cols + c, got0, got1, 0)

    ones = jnp.ones((8, BLK), BF)
    zero_block = jnp.zeros((BLK, C), BF)
    sums0[0] = jnp.zeros((FOLD, C), F32)
    sums1[0] = jnp.zeros((FOLD, C), F32)
    density_sums[0] = jnp.zeros((8, CELLS), F32)

    def folded(matrix, stream, i):
        other = swapped(stream).astype(BF)
        low, high = (stream, other) if i == 0 else (other, stream)
        right = jnp.concatenate([jnp.where(low_lanes, low, zero_block), jnp.where(low_lanes, zero_block, high)], axis=0)
        left = jnp.concatenate([matrix[:FOLD], matrix[FOLD:]], axis=1)
        return jnp.dot(left, right, preferred_element_type=F32)

    def receive0(j):
        metas = got0[j, BLK:, :].astype(F32)
        stream = got0[j, :BLK, :]
        for i in range(MOST):
            meta = metas[8 * i : 8 * i + 8]
            matrix = window_weights(meta)
            matrices[j * MOST + i] = matrix
            patch_rows[j * MOST + i] = jnp.broadcast_to(meta[4:5], (8, BLK))
            sums0[1 + j * MOST + i] = folded(matrix, stream, i)
            density_sums[1 + j * MOST + i] = lax.dot_general(ones, matrix, (((1,), (1,)), ((), ())), preferred_element_type=F32)

    def step0(p, carry):
        for j in (2 * p, 2 * p + 1):
            out_copy(0, j).wait_recv()
        for j in (2 * p, 2 * p + 1):
            receive0(j)
        return carry

    receive0(0)
    out_copy(0, 1).wait_recv()
    receive0(1)
    lax.fori_loop(1, tiles // 2, step0, 0)

    by_row = jnp.concatenate([patch_rows[s, 0:1, :] for s in range(slots)], axis=0)
    slot_row = lax.broadcasted_iota(jnp.int32, (slots, C), 0)
    lane = lax.broadcasted_iota(jnp.int32, (slots, C), 1)
    by_lane = jnp.sum(jnp.where(slot_row == lane, by_row, 0.0), axis=0, keepdims=True)
    earlier = jnp.max(jnp.where((by_row == by_lane) & (slot_row < lane), slot_row + 1, 0), axis=0, keepdims=True)
    latest = jnp.max(jnp.where(by_row == lane.astype(F32), slot_row + 1, 0), axis=0, keepdims=True)
    link_id = lax.broadcasted_iota(jnp.int32, (8, C), 0)
    ids = jnp.clip(by_lane.astype(jnp.int32), 0, ORBITS * PATCHES - 1)
    links[...] = jnp.where(link_id == 0, earlier, jnp.where(link_id == 1, latest, ids))
    link_copy = pltpu.make_async_copy(links, links_smem, link_sem)
    link_copy.start()
    link_copy.wait()

    def chain(s, carry):
        e = links_smem[0, s]
        sums0[s + 1] = sums0[s + 1] + sums0[e]
        density_sums[s + 1] = density_sums[s + 1] + density_sums[e]
        return carry

    lax.fori_loop(0, slots, chain, 0)

    for p in range(ORBITS * PATCHES):
        at = links_smem[1, p]
        owner, local_patch = p // PATCHES, p % PATCHES
        part0[owner, local_patch * FOLD : (local_patch + 1) * FOLD, :] = sums0[at].astype(BF)
        row = density_sums[at]
        density_rows[owner, local_patch : local_patch + 1, :] = row[0:1, :C]
        density_rows[owner, PATCHES + local_patch : PATCHES + local_patch + 1, :] = row[0:1, C:]
    for owner in range(ORBITS):
        density_part[owner] = density_rows[owner].astype(BF)
        part0[owner, PATCHES * FOLD :, :] = density_part[owner]

    cut = PATCHES * FOLD // 2
    parts = (part0, part1)

    def ring_copy(q, src, dst, way, step, other):
        return pltpu.make_async_remote_copy(
            src_ref=src, dst_ref=dst, send_sem=ring_send.at[q, way, step], recv_sem=ring_recv.at[q, way, step],
            device_id=(other, r, c), device_id_type=MESH,
        )

    def sides(q):
        low, high = pl.ds(0, cut), pl.ds(cut, cut + (DENS if q == 0 else 0))
        return ((0, after, low, high), (1, before, high, low))

    rings = {}

    def ring_start(q):
        rings[q] = []
        for way, other, passed, direct in sides(q):
            relay = ring_copy(q, parts[q].at[across, passed], relay_in.at[q, passed], way, 0, other)
            straight = ring_copy(q, parts[q].at[other, direct], part_in.at[q, way, direct], way, 1, other)
            summed = ring_copy(q, relay_out.at[q, passed], part_in.at[q, way, passed], way, 2, other)
            relay.start()
            straight.start()
            rings[q].append((relay, straight, summed))

    def ring_relay(q):
        for way, other, passed, direct in sides(q):
            relay, straight, summed = rings[q][way]
            relay.wait_recv()
            total = parts[q][other, passed].astype(F32) + relay_in[q, passed].astype(F32)
            relay_out[q, passed] = total.astype(BF)
            summed.start()

    def ring_finish(q):
        for relay, straight, summed in rings[q]:
            straight.wait_recv()
        for relay, straight, summed in rings[q]:
            summed.wait_recv()

    ring_start(0)

    def receive1(j):
        stream = got1[j]
        for i in range(MOST):
            s = j * MOST + i
            sums1[s + 1] = folded(matrices[s], stream, i) + sums1[links_smem[0, s]]

    def step1(p, carry):
        for j in (2 * p, 2 * p + 1):
            out_copy(1, j).wait_recv()
        for j in (2 * p, 2 * p + 1):
            receive1(j)
        return carry

    receive1(0)
    out_copy(1, 1).wait_recv()
    receive1(1)
    middle = max(1, tiles // 4)
    lax.fori_loop(1, middle, step1, 0)
    ring_relay(0)
    lax.fori_loop(middle, tiles // 2, step1, 0)
    for p in range(ORBITS * PATCHES):
        owner, local_patch = p // PATCHES, p % PATCHES
        part1[owner, local_patch * FOLD : (local_patch + 1) * FOLD, :] = sums1[links_smem[1, p]].astype(BF)
    ring_start(1)
    ring_finish(0)

    tail = pl.ds(PATCHES * FOLD, DENS)
    dens_in = jnp.concatenate([part0[z, tail], part_in[0, 0, tail], part_in[0, 1, tail]], axis=0)
    pick_shape = (3 * DENS, DENS * C)
    picked = lax.broadcasted_iota(jnp.int32, pick_shape, 0) % DENS == lax.broadcasted_iota(jnp.int32, pick_shape, 1) // C
    density_all = lax.dot_general(dens_in, picked.astype(BF), (((0,), (0,)), ((), ())), preferred_element_type=F32)
    weight_swapped = jnp.concatenate([dw_ref[:, HALF:], dw_ref[:, :HALF]], axis=1)
    low_row = lax.broadcasted_iota(jnp.int32, (1, C), 1) < HALF
    weights = (jnp.where(low_row, dw_ref[...], weight_swapped), jnp.where(low_row, weight_swapped, dw_ref[...]))

    def grid_value(q, p):
        cells = pl.ds(p * FOLD, FOLD)
        density = jnp.where(
            low_lanes, density_all[:, p * C : (p + 1) * C], density_all[:, (PATCHES + p) * C : (PATCHES + p + 1) * C]
        )
        total = parts[q][z, cells].astype(F32) + part_in[q, 0, cells].astype(F32) + part_in[q, 1, cells].astype(F32)
        return total / jnp.maximum(density, 1.0) + weights[q] * (density / (1.0 + density))

    for p in range(PATCHES):
        packed[p] = grid_value(0, p)
    ring_relay(1)
    ring_finish(1)
    for p in range(PATCHES):
        x0, x1 = packed[p], grid_value(1, p)
        top, left = p // WIDE * PH, p % WIDE * PW
        lower = jnp.where(low_lanes, x0, swapped(x1)).astype(BF)
        upper = jnp.where(low_lanes, swapped(x0), x1).astype(BF)
        tile[top : top + PH // 2, left : left + PW, :] = lower.reshape(PH // 2, PW, C)
        tile[top + PH // 2 : top + PH, left : left + PW, :] = upper.reshape(PH // 2, PW, C)

    def exchange(origin, turn):
        for i in range(SR):
            col_out[turn, 0, i : i + 1, :] = origin[i, 0:1, :]
            col_out[turn, 1, i : i + 1, :] = origin[i, TC - 1 : TC, :]
        copies = []
        for e, (up, side) in enumerate(edges):
            if side == 0:
                src, dst = origin.at[0 if up < 0 else SR - 1], row_in.at[turn, e]
            else:
                src, dst = col_out.at[turn, 0 if side < 0 else 1], col_in.at[turn, e - 2]
            copies.append(pltpu.make_async_remote_copy(
                src_ref=src, dst_ref=dst, send_sem=edge_send.at[turn, e], recv_sem=edge_recv.at[turn, e],
                device_id=edge_device(up, side), device_id_type=MESH,
            ))
        for copy in copies:
            copy.start()

        def shifts(row, centre):
            centre = centre.astype(F32)
            wide[row, :, 0:C] = pltpu.roll(centre, 1, 0).astype(BF)
            wide[row, :, C : 2 * C] = centre.astype(BF)
            wide[row, :, 2 * C :] = pltpu.roll(centre, TC - 1, 0).astype(BF)

        for i in range(SR):
            shifts(i + 1, origin[i])
        for copy in copies:
            copy.wait_recv()
        shifts(0, jnp.where(stripe > 0, row_in[turn, 1].astype(F32), 0.0))
        shifts(SR + 1, jnp.where(stripe < stripes - 1, row_in[turn, 0].astype(F32), 0.0))
        for first_edge, lanes, at, open_ in ((3, slice(0, C), 0, c > 0), (0, slice(2 * C, 3 * C), TC - 1, c < cols - 1)):
            above = col_in[turn, first_edge + 2, SR - 1 : SR, :].astype(F32)
            level = col_in[turn, first_edge + 1].astype(F32)
            below = col_in[turn, first_edge, 0:1, :].astype(F32)
            above = jnp.where(open_ & (stripe > 0), above, 0.0)
            level = jnp.where(open_, level, 0.0)
            below = jnp.where(open_ & (stripe < stripes - 1), below, 0.0)
            wide[0, at : at + 1, lanes] = above.astype(BF)
            wide[SR + 1, at : at + 1, lanes] = below.astype(BF)
            for i in range(SR):
                wide[i + 1, at : at + 1, lanes] = level[i : i + 1].astype(BF)
        return copies

    block_rows = PH // 2

    def convolved(i, w_ref, b_ref):
        total = None
        for a in range(3):
            x = wide[pl.ds(i + a, block_rows)].reshape(block_rows * TC, 3 * C)
            term = jnp.dot(x, w_ref[a], preferred_element_type=F32)
            total = term if total is None else total + term
        return total + b_ref[...]

    edge_copies = exchange(tile, 0)
    for i in range(0, SR, block_rows):
        v = convolved(i, w1_ref, b1_ref)
        first[i : i + block_rows] = (v / (1.0 + jnp.exp(-v))).astype(BF).reshape(block_rows, TC, C)
    edge_copies += exchange(first, 1)

    count = PATCHES // 2
    values = (values0, values1)

    def half_of(q, owner, h):
        return values[q].at[pl.ds(owner * PATCHES + h * count, count)]

    def gather_copy(q, owner, h, way, step, src):
        return pltpu.make_async_remote_copy(
            src_ref=src, dst_ref=half_of(q, owner, h), send_sem=gather_send.at[q, way, step],
            recv_sem=gather_recv.at[q, way, step], device_id=((after, before)[way], r, c), device_id_type=MESH,
        )

    gathers = []

    def gather_start(q, h):
        for way in range(2):
            copy = gather_copy(q, z, h, way, h, mine.at[q, pl.ds(h * count, count)])
            copy.start()
            gathers.append(copy)

    near = (before, after)

    def gather_relay(q):
        for way in range(2):
            gather_copy(q, near[way], way, way, way, half_of(q, near[way], way)).wait_recv()
            copy = gather_copy(q, near[way], way, way, 2, half_of(q, near[way], way))
            copy.start()
            gathers.append(copy)

    def gather_finish(q):
        for way in range(2):
            gather_copy(q, near[way], 1 - way, way, 1 - way, half_of(q, near[way], 1 - way)).wait_recv()
        for way in range(2):
            gather_copy(q, across, way, way, 2, half_of(q, across, way)).wait_recv()

    for h in range(2):
        halves = []
        for i in range(h * PH, (h + 1) * PH, block_rows):
            v = convolved(i, w2_ref, b2_ref).reshape(block_rows, TC, C)
            v = (tile[i : i + block_rows].astype(F32) + v).astype(BF)
            grid_ref[i : i + block_rows] = v
            halves.append(v)
        for w in range(WIDE):
            lower = halves[0][:, w * PW : (w + 1) * PW, :].reshape(FOLD, C)
            upper = halves[1][:, w * PW : (w + 1) * PW, :].reshape(FOLD, C)
            mine[0, h * count + w] = jnp.where(low_lanes, lower, swapped(upper).astype(BF))
            mine[1, h * count + w] = jnp.where(low_lanes, swapped(lower).astype(BF), upper)
        gather_start(0, h)
    for q in range(2):
        values[q][pl.ds(z * PATCHES, PATCHES)] = mine[q]
    gather_relay(0)
    gather_start(1, 0)
    gather_start(1, 1)
    gather_finish(0)

    def swap_values(q):
        def one(p, carry):
            values_swapped[q, p] = swapped(values[q][p]).astype(BF)
            return carry

        lax.fori_loop(0, ORBITS * PATCHES, one, 0)

    one_block = jnp.ones((BLK, C), BF)
    one_low, one_high = jnp.where(low_lanes, one_block, zero_block), jnp.where(low_lanes, zero_block, one_block)

    def read(q, j, target_ref):
        patches = [links_smem[2, j * MOST + i] for i in range(MOST)]
        a, b = patches
        low0 = jnp.where(low_lanes, values[q][a], zero_block)
        low1 = jnp.where(low_lanes, values_swapped[q, a], zero_block)
        high0 = jnp.where(low_lanes, zero_block, values_swapped[q, b])
        high1 = jnp.where(low_lanes, zero_block, values[q][b])
        right = jnp.concatenate([
            jnp.concatenate([low0, one_low], axis=1), jnp.concatenate([low1, one_low], axis=1),
            jnp.concatenate([high0, one_high], axis=1), jnp.concatenate([high1, one_high], axis=1),
        ], axis=0)
        left = jnp.concatenate([matrices[j * MOST], matrices[j * MOST + 1]], axis=0)
        summed = lax.dot_general(left, right, (((0,), (0,)), ((), ())), preferred_element_type=F32)
        total = jnp.where(summed[:, C:] > 0.0, summed[:, C:], 1.0)
        target_ref[q, j] = (summed[:, :C] / total).astype(BF)

    def back_copy(q, j):
        return pltpu.make_async_remote_copy(
            src_ref=back_out.at[q, j], dst_ref=back_in.at[q, j], send_sem=back_send.at[q, j], recv_sem=back_recv.at[q, j],
            device_id=(z, *source(j)), device_id_type=MESH,
        )

    def read_and_send(q):
        def step(j, carry):
            read(q, j, back_out)
            back_copy(q, j).start()
            return carry

        return step

    swap_values(0)
    lax.fori_loop(1, tiles // 2, read_and_send(0), 0)
    gather_relay(1)
    lax.fori_loop(tiles // 2, tiles, read_and_send(0), 0)
    read(0, 0, back_in)
    gather_finish(1)
    swap_values(1)
    lax.fori_loop(1, tiles, read_and_send(1), 0)
    read(1, 0, back_in)

    def arrive(q):
        def step(j, carry):
            back_copy(q, j).wait_recv()
            return carry

        return step

    lax.fori_loop(1, tiles, arrive(0), 0)
    lax.fori_loop(1, tiles, arrive(1), 0)

    def combine(b, carry):
        t = tile_of[b]
        k = (t // cols + rows - r) % rows * cols + (t % cols + cols - c) % cols
        j = jnp.where(k == 0, 0, (k - 1 + tiles - 1 - tiles // 2) % (tiles - 1) + 1)
        is_low = jnp.full((BLK, C), rank_of[b]) == 0
        x0, x1 = back_in[0, j].astype(F32), back_in[1, j].astype(F32)
        lower = jnp.where(is_low, x0, swapped(x0))
        upper = jnp.where(is_low, swapped(x1), x1)
        reading = jnp.where(low_lanes, lower, upper)
        out_ref[b] = (features[b].astype(F32) + reading).astype(BF)
        return carry

    lax.fori_loop(0, blocks, combine, 0)

    def sent(j, carry):
        for q in range(2):
            out_copy(q, j).wait_send()
            back_copy(q, j).wait_send()
        return carry

    lax.fori_loop(1, tiles, sent, 0)
    for q in range(2):
        for copies in rings[q]:
            for copy in copies:
                copy.wait_send()
    for copy in gathers + edge_copies:
        copy.wait_send()


def local(
    obs_feat, obs_offset, obs_cells, block_tile, block_patch, w_embed, b_embed, w_proj, b_proj, density_weight,
    w_first, b_first, w_second, b_second,
):
    blocks = block_tile.shape[0]
    rows, cols = lax.axis_size("rows"), lax.axis_size("cols")
    tiles = rows * cols
    slots = tiles * MOST
    patches = ORBITS * PATCHES

    vm = pl.BlockSpec(memory_space=VMEM)
    sm = pl.BlockSpec(memory_space=SMEM)
    block_at, patch_at, rank_of = pl.pallas_call(
        functools.partial(table_kernel, blocks, slots),
        out_shape=tuple(jax.ShapeDtypeStruct((n,), jnp.int32) for n in (slots, slots, blocks)),
        in_specs=[sm, sm],
        out_specs=(sm, sm, sm),
        scratch_shapes=[SMEM((tiles,), jnp.int32)],
        name="tables",
    )(block_tile, block_patch)

    part_rows = PATCHES * FOLD + DENS
    dma = pltpu.SemaphoreType.DMA
    obs_out, grid_out = pl.pallas_call(
        functools.partial(main_kernel, rows, cols, blocks),
        grid=(1,),
        out_shape=(jax.ShapeDtypeStruct((blocks, BLK, C), BF), jax.ShapeDtypeStruct((SR, TC, C), BF)),
        in_specs=[sm] * 4 + [vm, vm, pl.BlockSpec((8, blocks * BLK), lambda i: (0, 0))] + [vm] * 9,
        out_specs=(vm, vm),
        scratch_shapes=[
            VMEM((blocks, BLK, C), BF),
            VMEM((blocks, BLK, C), BF),
            VMEM((blocks, 8, BLK), F32),
            VMEM((tiles, BLK + META, C), BF),
            VMEM((tiles, BLK, C), BF),
            VMEM((tiles, BLK + META, C), BF),
            VMEM((tiles, BLK, C), BF),
            VMEM((slots, CELLS, BLK), BF),
            VMEM((slots, 8, BLK), F32),
            VMEM((slots + 1, FOLD, C), F32),
            VMEM((slots + 1, FOLD, C), F32),
            VMEM((slots + 1, 8, CELLS), F32),
            VMEM((8, C), jnp.int32),
            SMEM((8, C), jnp.int32),
            VMEM((ORBITS, DENS, C), F32),
            VMEM((ORBITS, part_rows, C), BF),
            VMEM((ORBITS, part_rows, C), BF),
            VMEM((ORBITS, DENS, C), BF),
            VMEM((2, part_rows, C), BF),
            VMEM((2, part_rows, C), BF),
            VMEM((2, 2, part_rows, C), BF),
            VMEM((PATCHES, FOLD, C), F32),
            VMEM((SR, TC, C), BF),
            VMEM((SR + 2, TC, 3 * C), BF),
            VMEM((SR, TC, C), BF),
            VMEM((2, 2, SR, C), BF),
            VMEM((2, 2, TC, C), BF),
            VMEM((2, 6, SR, C), BF),
            VMEM((2, PATCHES, FOLD, C), BF),
            VMEM((patches, FOLD, C), BF),
            VMEM((patches, FOLD, C), BF),
            VMEM((2, patches, FOLD, C), BF),
            VMEM((2, tiles, BLK, C), BF),
            VMEM((2, tiles, BLK, C), BF),
            dma((2, tiles)),
            dma((2, tiles)),
            dma((2, 2, 3)),
            dma((2, 2, 3)),
            dma((2, 8)),
            dma((2, 8)),
            dma((2, 2, 3)),
            dma((2, 2, 3)),
            dma((2, tiles)),
            dma((2, tiles)),
            dma,
        ],
        compiler_params=pltpu.CompilerParams(collective_id=0, has_side_effects=True, vmem_limit_bytes=63000000),
        name="encode",
    )(
        block_at, patch_at, block_tile, rank_of,
        obs_feat.reshape(blocks, BLK, C), obs_offset, obs_cells, w_embed, b_embed[None, :], w_proj, b_proj[None, :],
        density_weight[None, :], w_first.reshape(3, 3 * C, C), b_first[None, :], w_second.reshape(3, 3 * C, C), b_second[None, :],
    )
    return (obs_out.reshape(obs_feat.shape), grid_out)


def solution(mesh):
    by_device = P(("orbits", "rows", "cols"))
    in_specs = (
        P(("orbits", "rows", "cols"), None), P(None, ("orbits", "rows", "cols")), P(None, ("orbits", "rows", "cols")),
        by_device, by_device, P(), P(), P(), P(), P(), P(), P(), P(), P(),
    )
    out_specs = (P(("orbits", "rows", "cols"), None), P(("orbits", "rows"), "cols", None))
    return jax.shard_map(local, mesh=mesh, in_specs=in_specs, out_specs=out_specs, check_vma=False)
```

time: 258 us -> 116 us (0.45); the launches traced: 254 us -> 116 us
  waiting for transfers between devices: 96.5 us -> 0 us
  starting transfers between devices: 20.6 us -> 0 us
  Pallas kernels: 98.1 us -> 112 us
  between operations: 14.1 us -> 0.65 us
  other arithmetic: 9.67 us -> 0 us
  local copies, waits for them, and re-layouts: 11.4 us -> 3.12 us
  matrix products: 3.48 us -> 0 us
    reduce_scatter x2 -> x0, waiting for transfers between devices: 53.9 us -> none  [the longest x1 31.3 us: local(): lax.psum_scatter(spread_tile, 'orbits', scatter_dimension=0, tiled=True)]
    all_gather x1 -> x0, waiting for transfers between devices: 31 us -> none  [local(): full_out = lax.all_gather(grid_out, 'orbits', axis=0, tiled=True)]
    ppermute x8 -> x0, starting transfers between devices: 20.5 us -> none  [the longest x4 10.7 us: extended(): before = lax.ppermute(last, axis, up)]
    pallas_call x3 -> x2, Pallas kernels: 98.1 us -> 112 us  [the longest x1 110 us: local(): pl.pallas_call(functools.partial(main_kernel, rows, cols, blocks), grid=(...]
    ppermute x8 -> x0, waiting for transfers between devices: 11.6 us -> none  [the longest x4 11.5 us: extended(): after = lax.ppermute(initial, axis, down)]
    transpose x1 -> x0, local copies, waits for them, and re-layouts: 3.51 us -> none  [patches_to_tile(): shaped.transpose(axes_order).reshape((tile_height, tile_width) + trailing)]
    dot_general x6 -> x0, matrix products: 3.48 us -> none  [convolve(): jnp.dot(stacked.reshape(-1, 3 * channels), weight[row_shift].reshape(3 *...]
    convert_element_type x4 -> x0, other arithmetic: 3.35 us -> none  [the longest x1 1.66 us: local(): grid_in = (spread_part / jnp.maximum(density_part, 1.0)[..., None] + dens...]
  transfers between devices with their start and end apart: 11 -> 0, of which waited for: 7 -> 0; matrix products, arithmetic and copies ran while one was open for 2% -> 0% of each run, Pallas kernels for 0% -> 0%
where the time goes in v3:
time: 116 us
  Pallas kernels  112 us (97%)
  local copies, waits for them, and re-layouts  3.12 us (3%)
    pallas_call x1, Pallas kernels, local(): pl.pallas_call(functools.partial(main_kernel, rows, cols, blocks), grid=(...  110 us
    unnamed x4, local copies, waits for them, and re-layouts  3.12 us

profile of v3, /device:TPU:2, one launch (start us, length us, event | category | flops | bytes accessed | tf_op | source)
XLA Modules:
  0.0 115.7 jit_solution(12497383070709821806)
XLA Ops:
  0.6 2.3 %tables.1 = (s32[64]{0:T(128)}, s32[64]{0:T(128)}, s32[32]{0:T(128)}) custom-call(s32[32]{0:T(128)} %tile_of.1, s32[32]{0:T(128)} %patch_ref.1), custom_call_target="tpu_custom_call" | custom-call | tf_op jit(solution)/shard_map/tables/pallas_call | solution.py:559
  2.9 109.7 %encode.1 = (bf16[32,128,128]{2,1,0:T(8,128)(2,1)}, bf16[16,128,128]{2,1,0:T(8,128)(2,1)}) custom-call(s32[64]{0:T(128)} %get-tuple-element.7.block_at, s32[64]{0:T(128)} %get-tuple-element.8.patch_at, s32[32]{0:T(128)} %tile_of.1, s32[32]{0:T(128)} %get-tuple-element.9.rank_of, bf16[32,128,128]{2,1,0:T(8,128)(2,1)} %bitcast.9, bf16[2,4096]{1,0:T(2,128)(2,1)} %off_ref.1, ...), custom_call_target="tpu_custom_call" | custom-call | tf_op jit(solution)/shard_map/encode/pallas_call | solution.py:570
  112.6 0.0 copy-start
  112.6 2.3 %copy.18 = bf16[4096,128]{1,0:T(8,128)(2,1)} copy(bf16[4096,128]{1,0:T(8,128)(2,1)} %bitcast.10) | data formatting | bytes 2097152
  114.9 0.0 copy-done
  114.9 0.8 copy.19
Async XLA Ops:
  112.6 2.3 %copy-start = (bf16[16,128,128]{2,1,0:T(8,128)(2,1)S(1)}, bf16[16,128,128]{2,1,0:T(8,128)(2,1)}, u32[]{:S(2)}) copy-start(bf16[16,128,128]{2,1,0:T(8,128)(2,1)} %get-tuple-element.15) | copy-start | bytes 1572868

commit v4 on v3

--- a/solution.py
+++ b/solution.py
@@ -20,7 +20,8 @@
 WIDE = TC // PW
 PATCHES = SR // PH * WIDE
 DENS = 2 * PATCHES
-META = 16
+META = 8
+DEAD = -128.0
 ORBITS = 4
 MESH = pl.DeviceIdType.MESH
 VMEM = pltpu.VMEM
@@ -29,34 +30,10 @@
 F32 = jnp.float32
 
 
-def table_kernel(blocks, slots, tile_ref, patch_ref, block_at, patch_at, rank_of, count):
-    def clear(s, carry):
-        block_at[s] = 0
-        patch_at[s] = -1
-        return carry
-
-    def empty(t, carry):
-        count[t] = 0
-        return carry
-
-    lax.fori_loop(0, slots, clear, 0)
-    lax.fori_loop(0, slots // MOST, empty, 0)
-
-    def place(b, carry):
-        t = tile_ref[b]
-        rank = count[t]
-        count[t] = rank + 1
-        rank_of[b] = rank
-        block_at[t * MOST + rank] = b
-        patch_at[t * MOST + rank] = patch_ref[b]
-        return carry
-
-    lax.fori_loop(0, blocks, place, 0)
-
-
 def window_weights(meta_rows):
-    off_r, off_c = meta_rows[0:1], meta_rows[1:2]
-    anchor_r, anchor_c = meta_rows[2:3], meta_rows[3:4]
+    off_r, off_c, anchor = meta_rows[0:1], meta_rows[1:2], meta_rows[2:3]
+    anchor_r = jnp.floor(anchor * (1.0 / PW))
+    anchor_c = anchor - anchor_r * PW
     tap_r = lax.broadcasted_iota(jnp.int32, (PH, BLK), 0).astype(F32) - anchor_r
     tap_c = lax.broadcasted_iota(jnp.int32, (PW, BLK), 0).astype(F32) - anchor_c
     delta_r = tap_r - 1.5 - off_r
@@ -72,13 +49,14 @@
 
 def main_kernel(
     rows, cols, blocks,
-    block_at, patch_at, tile_of, rank_of,
-    feat_ref, off_ref, cells_ref, we_ref, be_ref, wp_ref, bp_ref, dw_ref, w1_ref, b1_ref, w2_ref, b2_ref,
+    tile_of, tile_row, patch_row, feat_hbm, off_hbm, cells_hbm, w1_hbm, w2_hbm,
+    we_ref, be_ref, wp_ref, bp_ref, dw_ref, b1_ref, b2_ref,
     out_ref, grid_ref,
+    feat_ref, off_ref, cells_ref, w1_ref, w2_ref, table, table_smem,
     features, swapped_features, block_meta, send0, send1, got0, got1, matrices, patch_rows,
     sums0, sums1, density_sums, links, links_smem, density_rows, part0, part1, density_part, relay_in, relay_out, part_in,
-    packed, tile, wide, first, col_out, row_in, col_in, mine, values0, values1, values_swapped, back_out, back_in,
-    out_send, out_recv, ring_send, ring_recv, edge_send, edge_recv, gather_send, gather_recv, back_send, back_recv, link_sem,
+    packed, tile, wide, first, col_out, row_in, col_in, mine, values0, values1, values_swapped, back_out, back0, back1,
+    out_send, out_recv, ring_send, ring_recv, edge_send, edge_recv, gather_send, gather_recv, back_send, back_recv, link_sem, load_sem,
 ):
     z, r, c = lax.axis_index("orbits"), lax.axis_index("rows"), lax.axis_index("cols")
     tiles = rows * cols
@@ -116,7 +94,34 @@
     for up, side in edges:
         pl.semaphore_signal(barrier, inc=1, device_id=edge_device(up, side), device_id_type=MESH)
 
-    group = min(4, blocks)
+    half_blocks = blocks // 2
+    loads = [
+        pltpu.make_async_copy(feat_hbm.at[pl.ds(0, half_blocks)], feat_ref.at[pl.ds(0, half_blocks)], load_sem.at[0]),
+        pltpu.make_async_copy(feat_hbm.at[pl.ds(half_blocks, half_blocks)], feat_ref.at[pl.ds(half_blocks, half_blocks)], load_sem.at[1]),
+        pltpu.make_async_copy(off_hbm, off_ref, load_sem.at[2]),
+        pltpu.make_async_copy(cells_hbm.at[pl.ds(0, 8)], cells_ref, load_sem.at[3]),
+        pltpu.make_async_copy(w1_hbm, w1_ref, load_sem.at[4]),
+        pltpu.make_async_copy(w2_hbm, w2_ref, load_sem.at[5]),
+    ]
+    for load in loads:
+        load.start()
+
+    square = (tiles, blocks)
+    block_id = lax.broadcasted_iota(jnp.int32, square, 1).astype(F32)
+    hit = tile_row[...] == lax.broadcasted_iota(jnp.int32, square, 0)
+    lowest = jnp.min(jnp.where(hit, block_id, float(blocks)), axis=1, keepdims=True)
+    highest = jnp.max(jnp.where(hit, block_id, -1.0), axis=1, keepdims=True)
+    row_patches = patch_row[...].astype(F32)
+    patch_low = jnp.max(jnp.where(block_id == lowest, row_patches, -1.0), axis=1, keepdims=True)
+    patch_high = jnp.max(jnp.where((block_id == highest) & (highest > lowest), row_patches, -1.0), axis=1, keepdims=True)
+    entry = lax.broadcasted_iota(jnp.int32, (tiles, C), 1)
+    found = jnp.where(entry == 0, lowest, jnp.where(entry == 1, highest, jnp.where(entry == 2, patch_low, patch_high)))
+    found = found.astype(jnp.int32)
+    table[...] = jnp.where(entry < 2, jnp.clip(found, 0, blocks - 1), found)
+    table_copy = pltpu.make_async_copy(table, table_smem, link_sem.at[1])
+    table_copy.start()
+
+    group = min(4, half_blocks)
     proj = jnp.concatenate([wp_ref[...], swapped(wp_ref[...]).astype(BF)], axis=1)
     proj_bias = jnp.concatenate([bp_ref[...], jnp.concatenate([bp_ref[:, HALF:], bp_ref[:, :HALF]], axis=1)], axis=1)
 
@@ -130,29 +135,31 @@
         swapped_features[at] = both[:, C:].reshape(group, BLK, C)
         return carry
 
-    lax.fori_loop(0, blocks // group, embed, 0)
+    loads[0].wait()
+    lax.fori_loop(0, half_blocks // group, embed, 0)
+    loads[1].wait()
+    lax.fori_loop(half_blocks // group, blocks // group, embed, 0)
+    loads[2].wait()
+    loads[3].wait()
     row_id = lax.broadcasted_iota(jnp.int32, (8, BLK), 0)
+    row_kind = row_id % 4
     for b in range(blocks):
         lanes = slice(b * BLK, (b + 1) * BLK)
         off = off_ref[:, lanes].astype(F32)
-        cell = cells_ref[0:1, lanes]
-        meta = jnp.where(row_id == 0, off[0:1], 0.0)
-        meta = jnp.where(row_id == 1, off[1:2], meta)
-        meta = jnp.where(row_id == 2, (cell >> 5).astype(F32), meta)
-        block_meta[b] = jnp.where(row_id == 3, (cell & 31).astype(F32), meta)
+        meta = jnp.where(row_kind == 0, off[0:1], off[1:2])
+        block_meta[b] = jnp.where(row_kind == 2, cells_ref[0:1, lanes].astype(F32), meta)
+    table_copy.wait()
 
     low_lanes = lax.broadcasted_iota(jnp.int32, (BLK, C), 1) < HALF
 
     def pack(t, dst0, dst1, j):
-        at = [block_at[t * MOST + i] for i in range(MOST)]
+        at = [table_smem[t, i] for i in range(MOST)]
         dst0[j, :BLK, :] = jnp.where(low_lanes, features[at[0]], swapped_features[at[1]])
         dst1[j] = jnp.where(low_lanes, swapped_features[at[0]], features[at[1]])
-        metas = []
-        for i in range(MOST):
-            patch = jnp.full((8, BLK), patch_at[t * MOST + i].astype(F32))
-            meta = jnp.where((row_id == 2) & (patch < 0.0), -100.0, block_meta[at[i]])
-            metas.append(jnp.where(row_id == 4, patch, meta))
-        dst0[j, BLK:, :] = jnp.concatenate(metas, axis=0).astype(BF)
+        patch = jnp.where(row_id < 4, table_smem[t, 2].astype(F32), table_smem[t, 3].astype(F32))
+        meta = jnp.where(row_id < 4, block_meta[at[0]], block_meta[at[1]])
+        meta = jnp.where((row_kind == 2) & (patch < 0.0), DEAD, meta)
+        dst0[j, BLK:, :] = jnp.where(row_kind == 3, patch, meta).astype(BF)
 
     sends, gots = (send0, send1), (got0, got1)
 
@@ -195,10 +202,10 @@
         metas = got0[j, BLK:, :].astype(F32)
         stream = got0[j, :BLK, :]
         for i in range(MOST):
-            meta = metas[8 * i : 8 * i + 8]
+            meta = metas[4 * i : 4 * i + 4]
             matrix = window_weights(meta)
             matrices[j * MOST + i] = matrix
-            patch_rows[j * MOST + i] = jnp.broadcast_to(meta[4:5], (8, BLK))
+            patch_rows[j * MOST + i] = jnp.broadcast_to(meta[3:4], (8, BLK))
             sums0[1 + j * MOST + i] = folded(matrix, stream, i)
             density_sums[1 + j * MOST + i] = lax.dot_general(ones, matrix, (((1,), (1,)), ((), ())), preferred_element_type=F32)
 
@@ -223,7 +230,7 @@
     link_id = lax.broadcasted_iota(jnp.int32, (8, C), 0)
     ids = jnp.clip(by_lane.astype(jnp.int32), 0, ORBITS * PATCHES - 1)
     links[...] = jnp.where(link_id == 0, earlier, jnp.where(link_id == 1, latest, ids))
-    link_copy = pltpu.make_async_copy(links, links_smem, link_sem)
+    link_copy = pltpu.make_async_copy(links, links_smem, link_sem.at[0])
     link_copy.start()
     link_copy.wait()
 
@@ -395,6 +402,8 @@
         return total + b_ref[...]
 
     edge_copies = exchange(tile, 0)
+    loads[4].wait()
+    loads[5].wait()
     for i in range(0, SR, block_rows):
         v = convolved(i, w1_ref, b1_ref)
         first[i : i + block_rows] = (v / (1.0 + jnp.exp(-v))).astype(BF).reshape(block_rows, TC, C)
@@ -479,17 +488,19 @@
         left = jnp.concatenate([matrices[j * MOST], matrices[j * MOST + 1]], axis=0)
         summed = lax.dot_general(left, right, (((0,), (0,)), ((), ())), preferred_element_type=F32)
         total = jnp.where(summed[:, C:] > 0.0, summed[:, C:], 1.0)
-        target_ref[q, j] = (summed[:, :C] / total).astype(BF)
+        target_ref[j] = (summed[:, :C] / total).astype(BF)
+
+    back = (back0, back1)
 
     def back_copy(q, j):
         return pltpu.make_async_remote_copy(
-            src_ref=back_out.at[q, j], dst_ref=back_in.at[q, j], send_sem=back_send.at[q, j], recv_sem=back_recv.at[q, j],
+            src_ref=back_out.at[q, j], dst_ref=back[q].at[j], send_sem=back_send.at[q, j], recv_sem=back_recv.at[q, j],
             device_id=(z, *source(j)), device_id_type=MESH,
         )
 
     def read_and_send(q):
         def step(j, carry):
-            read(q, j, back_out)
+            read(q, j, back_out.at[q])
             back_copy(q, j).start()
             return carry
 
@@ -499,11 +510,11 @@
     lax.fori_loop(1, tiles // 2, read_and_send(0), 0)
     gather_relay(1)
     lax.fori_loop(tiles // 2, tiles, read_and_send(0), 0)
-    read(0, 0, back_in)
+    read(0, 0, back0)
     gather_finish(1)
     swap_values(1)
     lax.fori_loop(1, tiles, read_and_send(1), 0)
-    read(1, 0, back_in)
+    read(1, 0, back1)
 
     def arrive(q):
         def step(j, carry):
@@ -512,22 +523,26 @@
 
         return step
 
-    lax.fori_loop(1, tiles, arrive(0), 0)
-    lax.fori_loop(1, tiles, arrive(1), 0)
-
-    def combine(b, carry):
-        t = tile_of[b]
-        k = (t // cols + rows - r) % rows * cols + (t % cols + cols - c) % cols
-        j = jnp.where(k == 0, 0, (k - 1 + tiles - 1 - tiles // 2) % (tiles - 1) + 1)
-        is_low = jnp.full((BLK, C), rank_of[b]) == 0
-        x0, x1 = back_in[0, j].astype(F32), back_in[1, j].astype(F32)
-        lower = jnp.where(is_low, x0, swapped(x0))
-        upper = jnp.where(is_low, swapped(x1), x1)
-        reading = jnp.where(low_lanes, lower, upper)
-        out_ref[b] = (features[b].astype(F32) + reading).astype(BF)
-        return carry
-
-    lax.fori_loop(0, blocks, combine, 0)
+    together = min(4, blocks)
+
+    def combine(q):
+        def step(i, carry):
+            for u in range(together):
+                b = i * together + u
+                t = tile_of[b]
+                k = (t // cols + rows - r) % rows * cols + (t % cols + cols - c) % cols
+                j = jnp.where(k == 0, 0, (k - 1 + tiles - 1 - tiles // 2) % (tiles - 1) + 1)
+                in_place = jnp.full((BLK, C), (table_smem[t, 0] == b).astype(jnp.int32)) == 1 - q
+                x = back[q][j].astype(F32)
+                value = (features[b].astype(F32) + jnp.where(in_place, x, swapped(x))).astype(BF)
+                out_ref[b] = value if q == 0 else jnp.where(low_lanes, out_ref[b], value)
+            return carry
+
+        return step
+
+    for q in range(2):
+        lax.fori_loop(1, tiles, arrive(q), 0)
+        lax.fori_loop(0, blocks // together, combine(q), 0)
 
     def sent(j, carry):
         for q in range(2):
@@ -556,24 +571,22 @@
 
     vm = pl.BlockSpec(memory_space=VMEM)
     sm = pl.BlockSpec(memory_space=SMEM)
-    block_at, patch_at, rank_of = pl.pallas_call(
-        functools.partial(table_kernel, blocks, slots),
-        out_shape=tuple(jax.ShapeDtypeStruct((n,), jnp.int32) for n in (slots, slots, blocks)),
-        in_specs=[sm, sm],
-        out_specs=(sm, sm, sm),
-        scratch_shapes=[SMEM((tiles,), jnp.int32)],
-        name="tables",
-    )(block_tile, block_patch)
-
     part_rows = PATCHES * FOLD + DENS
     dma = pltpu.SemaphoreType.DMA
     obs_out, grid_out = pl.pallas_call(
         functools.partial(main_kernel, rows, cols, blocks),
         grid=(1,),
         out_shape=(jax.ShapeDtypeStruct((blocks, BLK, C), BF), jax.ShapeDtypeStruct((SR, TC, C), BF)),
-        in_specs=[sm] * 4 + [vm, vm, pl.BlockSpec((8, blocks * BLK), lambda i: (0, 0))] + [vm] * 9,
+        in_specs=[sm, vm, vm] + [pl.BlockSpec(memory_space=pl.ANY)] * 5 + [vm] * 7,
         out_specs=(vm, vm),
         scratch_shapes=[
+            VMEM((blocks, BLK, C), BF),
+            VMEM((2, blocks * BLK), BF),
+            VMEM((8, blocks * BLK), jnp.int32),
+            VMEM((3, 3 * C, C), BF),
+            VMEM((3, 3 * C, C), BF),
+            VMEM((tiles, C), jnp.int32),
+            SMEM((tiles, C), jnp.int32),
             VMEM((blocks, BLK, C), BF),
             VMEM((blocks, BLK, C), BF),
             VMEM((blocks, 8, BLK), F32),
@@ -607,7 +620,8 @@
             VMEM((patches, FOLD, C), BF),
             VMEM((2, patches, FOLD, C), BF),
             VMEM((2, tiles, BLK, C), BF),
-            VMEM((2, tiles, BLK, C), BF),
+            VMEM((tiles, BLK, C), BF),
+            VMEM((tiles, BLK, C), BF),
             dma((2, tiles)),
             dma((2, tiles)),
             dma((2, 2, 3)),
@@ -618,14 +632,15 @@
             dma((2, 2, 3)),
             dma((2, tiles)),
             dma((2, tiles)),
-            dma,
+            dma((2,)),
+            dma((6,)),
         ],
         compiler_params=pltpu.CompilerParams(collective_id=0, has_side_effects=True, vmem_limit_bytes=63000000),
         name="encode",
     )(
-        block_at, patch_at, block_tile, rank_of,
-        obs_feat.reshape(blocks, BLK, C), obs_offset, obs_cells, w_embed, b_embed[None, :], w_proj, b_proj[None, :],
-        density_weight[None, :], w_first.reshape(3, 3 * C, C), b_first[None, :], w_second.reshape(3, 3 * C, C), b_second[None, :],
+        block_tile, block_tile[None, :], block_patch[None, :], obs_feat.reshape(blocks, BLK, C), obs_offset, obs_cells,
+        w_first.reshape(3, 3 * C, C), w_second.reshape(3, 3 * C, C), w_embed, b_embed[None, :], w_proj, b_proj[None, :],
+        density_weight[None, :], b_first[None, :], b_second[None, :],
     )
     return (obs_out.reshape(obs_feat.shape), grid_out)
 

time: 116 us -> 111 us (0.957)
  Pallas kernels: 112 us -> 107 us
    pallas_call x1, Pallas kernels: 110 us -> 107 us  [local(): pl.pallas_call(functools.partial(main_kernel, rows, cols, blocks), grid=(...]
    pallas_call x1 -> x0, Pallas kernels: 2.28 us -> none  [local(): pl.pallas_call(functools.partial(table_kernel, blocks, slots), out_shape=...]
where the time goes in v4:
time: 111 us; the launch traced here: 110 us
  Pallas kernels  107 us (96%)
  local copies, waits for them, and re-layouts  3.12 us (3%)
    pallas_call x1, Pallas kernels, local(): pl.pallas_call(functools.partial(main_kernel, rows, cols, blocks), grid=(...  107 us
    unnamed x4, local copies, waits for them, and re-layouts  3.12 us

profile of v4, /device:TPU:2, one launch (start us, length us, event | category | flops | bytes accessed | tf_op | source)
XLA Modules:
  0.0 110.4 jit_solution(8895918223153910557)
XLA Ops:
  0.6 106.6 %encode.1 = (bf16[32,128,128]{2,1,0:T(8,128)(2,1)}, bf16[16,128,128]{2,1,0:T(8,128)(2,1)}) custom-call(s32[32]{0:T(128)} %tile_of.1, s32[1,32]{1,0:T(1,128)} %bitcast.15, s32[1,32]{1,0:T(1,128)} %bitcast.16, bf16[32,128,128]{2,1,0:T(8,128)(2,1)} %bitcast.12, bf16[2,4096]{1,0:T(2,128)(2,1)} %off_hbm.1, s32[16,4096]{1,0:T(8,128)} %cells_hbm.1, ...), custom_call_target="tpu_custom_call" | custom-call | tf_op jit(solution)/shard_map/encode/pallas_call | solution.py:576
  107.3 0.0 copy-start
  107.3 2.3 %copy.18 = bf16[4096,128]{1,0:T(8,128)(2,1)} copy(bf16[4096,128]{1,0:T(8,128)(2,1)} %bitcast.11) | data formatting | bytes 2097152
  109.6 0.0 copy-done
  109.6 0.8 copy.19
Async XLA Ops:
  107.3 2.3 %copy-start = (bf16[16,128,128]{2,1,0:T(8,128)(2,1)S(1)}, bf16[16,128,128]{2,1,0:T(8,128)(2,1)}, u32[]{:S(2)}) copy-start(bf16[16,128,128]{2,1,0:T(8,128)(2,1)} %get-tuple-element.9) | copy-start | bytes 1572868

commit v5 on v4

--- a/solution.py
+++ b/solution.py
@@ -51,12 +51,12 @@
     rows, cols, blocks,
     tile_of, tile_row, patch_row, feat_hbm, off_hbm, cells_hbm, w1_hbm, w2_hbm,
     we_ref, be_ref, wp_ref, bp_ref, dw_ref, b1_ref, b2_ref,
-    out_ref, grid_ref,
-    feat_ref, off_ref, cells_ref, w1_ref, w2_ref, table, table_smem,
+    out_hbm, grid_hbm,
+    out_ref, grid_ref, feat_ref, off_ref, cells_ref, w1_ref, w2_ref, table, table_smem,
     features, swapped_features, block_meta, send0, send1, got0, got1, matrices, patch_rows,
-    sums0, sums1, density_sums, links, links_smem, density_rows, part0, part1, density_part, relay_in, relay_out, part_in,
-    packed, tile, wide, first, col_out, row_in, col_in, mine, values0, values1, values_swapped, back_out, back0, back1,
-    out_send, out_recv, ring_send, ring_recv, edge_send, edge_recv, gather_send, gather_recv, back_send, back_recv, link_sem, load_sem,
+    turned, inverse, sums0, sums1, density_sums, links, links_smem, density_rows, part0, part1, density_part, relay_in, relay_out, part_in,
+    packed, tile, wide, first, side_in, side_first, col_out, row_in, col_in, mine, values0, values1, values_swapped, back_out, back0, back1,
+    out_send, out_recv, ring_send, ring_recv, edge_send, edge_recv, gather_send, gather_recv, back_send, back_recv, link_sem, load_sem, store_sem, grid_sem,
 ):
     z, r, c = lax.axis_index("orbits"), lax.axis_index("rows"), lax.axis_index("cols")
     tiles = rows * cols
@@ -209,17 +209,20 @@
             sums0[1 + j * MOST + i] = folded(matrix, stream, i)
             density_sums[1 + j * MOST + i] = lax.dot_general(ones, matrix, (((1,), (1,)), ((), ())), preferred_element_type=F32)
 
+    unroll = min(4, tiles // 2)
+
     def step0(p, carry):
-        for j in (2 * p, 2 * p + 1):
-            out_copy(0, j).wait_recv()
-        for j in (2 * p, 2 * p + 1):
-            receive0(j)
-        return carry
-
-    receive0(0)
-    out_copy(0, 1).wait_recv()
-    receive0(1)
-    lax.fori_loop(1, tiles // 2, step0, 0)
+        for u in range(unroll):
+            out_copy(0, p * unroll + u).wait_recv()
+        for u in range(unroll):
+            receive0(p * unroll + u)
+        return carry
+
+    for u in range(1, unroll):
+        out_copy(0, u).wait_recv()
+    for u in range(unroll):
+        receive0(u)
+    lax.fori_loop(1, tiles // unroll, step0, 0)
 
     by_row = jnp.concatenate([patch_rows[s, 0:1, :] for s in range(slots)], axis=0)
     slot_row = lax.broadcasted_iota(jnp.int32, (slots, C), 0)
@@ -268,15 +271,16 @@
 
     rings = {}
 
-    def ring_start(q):
-        rings[q] = []
-        for way, other, passed, direct in sides(q):
-            relay = ring_copy(q, parts[q].at[across, passed], relay_in.at[q, passed], way, 0, other)
-            straight = ring_copy(q, parts[q].at[other, direct], part_in.at[q, way, direct], way, 1, other)
-            summed = ring_copy(q, relay_out.at[q, passed], part_in.at[q, way, passed], way, 2, other)
-            relay.start()
-            straight.start()
-            rings[q].append((relay, straight, summed))
+    def ring_start(q, which):
+        if q not in rings:
+            rings[q] = []
+            for way, other, passed, direct in sides(q):
+                relay = ring_copy(q, parts[q].at[across, passed], relay_in.at[q, passed], way, 0, other)
+                straight = ring_copy(q, parts[q].at[other, direct], part_in.at[q, way, direct], way, 1, other)
+                summed = ring_copy(q, relay_out.at[q, passed], part_in.at[q, way, passed], way, 2, other)
+                rings[q].append((relay, straight, summed))
+        for relay, straight, summed in rings[q]:
+            (relay if which == "relay" else straight).start()
 
     def ring_relay(q):
         for way, other, passed, direct in sides(q):
@@ -292,7 +296,8 @@
         for relay, straight, summed in rings[q]:
             summed.wait_recv()
 
-    ring_start(0)
+    ring_start(0, "relay")
+    ring_start(0, "straight")
 
     def receive1(j):
         stream = got1[j]
@@ -314,11 +319,30 @@
     lax.fori_loop(1, middle, step1, 0)
     ring_relay(0)
     lax.fori_loop(middle, tiles // 2, step1, 0)
-    for p in range(ORBITS * PATCHES):
-        owner, local_patch = p // PATCHES, p % PATCHES
-        part1[owner, local_patch * FOLD : (local_patch + 1) * FOLD, :] = sums1[links_smem[1, p]].astype(BF)
-    ring_start(1)
+    def fill_part1(owner):
+        for p in range(PATCHES):
+            part1[owner, p * FOLD : (p + 1) * FOLD, :] = sums1[links_smem[1, owner * PATCHES + p]].astype(BF)
+
+    fill_part1(across)
+    ring_start(1, "relay")
+    fill_part1(after)
+    fill_part1(before)
+    ring_start(1, "straight")
+    fill_part1(z)
     ring_finish(0)
+
+    zero_lanes = jnp.zeros((CELLS, C), BF)
+    one_cells = jnp.ones((CELLS, C), BF)
+    cell_low = lax.broadcasted_iota(jnp.int32, (CELLS, C), 1) < HALF
+    one_pair = jnp.concatenate([jnp.where(cell_low, one_cells, zero_lanes), jnp.where(cell_low, zero_lanes, one_cells)], axis=0)
+
+    def prepare(j, carry):
+        turned[j] = jnp.concatenate([matrices[j * MOST].T, matrices[j * MOST + 1].T], axis=1)
+        total = jnp.dot(turned[j], one_pair, preferred_element_type=F32)
+        inverse[j] = 1.0 / jnp.where(total > 0.0, total, 1.0)
+        return carry
+
+    quarter = max(1, tiles // 4)
 
     tail = pl.ds(PATCHES * FOLD, DENS)
     dens_in = jnp.concatenate([part0[z, tail], part_in[0, 0, tail], part_in[0, 1, tail]], axis=0)
@@ -339,7 +363,9 @@
 
     for p in range(PATCHES):
         packed[p] = grid_value(0, p)
+    lax.fori_loop(0, quarter, prepare, 0)
     ring_relay(1)
+    lax.fori_loop(quarter, 2 * quarter, prepare, 0)
     ring_finish(1)
     for p in range(PATCHES):
         x0, x1 = packed[p], grid_value(1, p)
@@ -349,65 +375,88 @@
         tile[top : top + PH // 2, left : left + PW, :] = lower.reshape(PH // 2, PW, C)
         tile[top + PH // 2 : top + PH, left : left + PW, :] = upper.reshape(PH // 2, PW, C)
 
-    def exchange(origin, turn):
-        for i in range(SR):
-            col_out[turn, 0, i : i + 1, :] = origin[i, 0:1, :]
-            col_out[turn, 1, i : i + 1, :] = origin[i, TC - 1 : TC, :]
-        copies = []
-        for e, (up, side) in enumerate(edges):
-            if side == 0:
-                src, dst = origin.at[0 if up < 0 else SR - 1], row_in.at[turn, e]
-            else:
-                src, dst = col_out.at[turn, 0 if side < 0 else 1], col_in.at[turn, e - 2]
-            copies.append(pltpu.make_async_remote_copy(
-                src_ref=src, dst_ref=dst, send_sem=edge_send.at[turn, e], recv_sem=edge_recv.at[turn, e],
-                device_id=edge_device(up, side), device_id_type=MESH,
-            ))
-        for copy in copies:
-            copy.start()
-
-        def shifts(row, centre):
-            centre = centre.astype(F32)
-            wide[row, :, 0:C] = pltpu.roll(centre, 1, 0).astype(BF)
-            wide[row, :, C : 2 * C] = centre.astype(BF)
-            wide[row, :, 2 * C :] = pltpu.roll(centre, TC - 1, 0).astype(BF)
-
-        for i in range(SR):
-            shifts(i + 1, origin[i])
-        for copy in copies:
-            copy.wait_recv()
-        shifts(0, jnp.where(stripe > 0, row_in[turn, 1].astype(F32), 0.0))
-        shifts(SR + 1, jnp.where(stripe < stripes - 1, row_in[turn, 0].astype(F32), 0.0))
-        for first_edge, lanes, at, open_ in ((3, slice(0, C), 0, c > 0), (0, slice(2 * C, 3 * C), TC - 1, c < cols - 1)):
-            above = col_in[turn, first_edge + 2, SR - 1 : SR, :].astype(F32)
-            level = col_in[turn, first_edge + 1].astype(F32)
-            below = col_in[turn, first_edge, 0:1, :].astype(F32)
-            above = jnp.where(open_ & (stripe > 0), above, 0.0)
-            level = jnp.where(open_, level, 0.0)
-            below = jnp.where(open_ & (stripe < stripes - 1), below, 0.0)
-            wide[0, at : at + 1, lanes] = above.astype(BF)
-            wide[SR + 1, at : at + 1, lanes] = below.astype(BF)
-            for i in range(SR):
-                wide[i + 1, at : at + 1, lanes] = level[i : i + 1].astype(BF)
-        return copies
-
-    block_rows = PH // 2
-
-    def convolved(i, w_ref, b_ref):
+    for i in range(SR):
+        for k in range(2):
+            col_out[0, k, i : i + 1, :] = tile[i, k : k + 1, :]
+            col_out[1, k, i : i + 1, :] = tile[i, TC - 2 + k : TC - 1 + k, :]
+    edge_copies = []
+    for e, (up, side) in enumerate(edges):
+        if side == 0:
+            src, dst = tile.at[pl.ds(0 if up < 0 else SR - 2, 2)], row_in.at[e]
+        else:
+            src, dst = col_out.at[0 if side < 0 else 1], col_in.at[e - 2]
+        edge_copies.append(pltpu.make_async_remote_copy(
+            src_ref=src, dst_ref=dst, send_sem=edge_send.at[e], recv_sem=edge_recv.at[e],
+            device_id=edge_device(up, side), device_id_type=MESH,
+        ))
+    for copy in edge_copies:
+        copy.start()
+
+    def shifts(row, centre):
+        centre = centre.astype(F32)
+        wide[row, :, 0:C] = pltpu.roll(centre, 1, 0).astype(BF)
+        wide[row, :, C : 2 * C] = centre.astype(BF)
+        wide[row, :, 2 * C :] = pltpu.roll(centre, TC - 1, 0).astype(BF)
+
+    def convolved(i, height, w_ref, b_ref):
         total = None
         for a in range(3):
-            x = wide[pl.ds(i + a, block_rows)].reshape(block_rows * TC, 3 * C)
+            x = wide[pl.ds(i + a, height)].reshape(height * TC, 3 * C)
             term = jnp.dot(x, w_ref[a], preferred_element_type=F32)
             total = term if total is None else total + term
         return total + b_ref[...]
 
-    edge_copies = exchange(tile, 0)
+    def silu(v):
+        return v / (1.0 + jnp.exp(-v))
+
+    for i in range(SR):
+        shifts(i + 2, tile[i])
     loads[4].wait()
     loads[5].wait()
-    for i in range(0, SR, block_rows):
-        v = convolved(i, w1_ref, b1_ref)
-        first[i : i + block_rows] = (v / (1.0 + jnp.exp(-v))).astype(BF).reshape(block_rows, TC, C)
-    edge_copies += exchange(first, 1)
+    for copy in edge_copies:
+        copy.wait_recv()
+    has_above, has_below = stripe > 0, stripe < stripes - 1
+    for k in range(2):
+        shifts(k, jnp.where(has_above, row_in[1, k].astype(F32), 0.0))
+        shifts(SR + 2 + k, jnp.where(has_below, row_in[0, k].astype(F32), 0.0))
+    for s, (first_edge, open_) in enumerate(((3, c > 0), (0, c < cols - 1))):
+        own_at, own_lanes = (0, slice(2 * C, 3 * C)) if s == 0 else (TC - 1, slice(0, C))
+        side_in[s, 2 : SR + 2, own_lanes] = col_out[s, s].astype(F32)
+        for k in range(2):
+            side_in[s, k : k + 1, own_lanes] = jnp.where(has_above, row_in[1, k, own_at : own_at + 1, :].astype(F32), 0.0)
+            side_in[s, SR + 2 + k : SR + 3 + k, own_lanes] = jnp.where(has_below, row_in[0, k, own_at : own_at + 1, :].astype(F32), 0.0)
+            lanes = slice((k + s) * C, (k + s + 1) * C)
+            above = col_in[first_edge + 2, k].astype(F32)[SR - 2 :]
+            below = col_in[first_edge, k].astype(F32)[:2]
+            side_in[s, 0:2, lanes] = jnp.where(open_ & has_above, above, 0.0)
+            side_in[s, 2 : SR + 2, lanes] = jnp.where(open_, col_in[first_edge + 1, k].astype(F32), 0.0)
+            side_in[s, SR + 2 : SR + 4, lanes] = jnp.where(open_ & has_below, below, 0.0)
+    for i in range(SR + 4):
+        wide[i, 0:1, 0:C] = side_in[0, i : i + 1, C : 2 * C].astype(BF)
+        wide[i, TC - 1 : TC, 2 * C :] = side_in[1, i : i + 1, C : 2 * C].astype(BF)
+
+    tall = 6
+    for i in range(0, SR + 2, tall):
+        first[i : i + tall] = silu(convolved(i, tall, w1_ref, b1_ref)).astype(BF).reshape(tall, TC, C)
+    side_row = lax.broadcasted_iota(jnp.int32, (SR + 2, C), 0)
+    inside = ((side_row > 0) | has_above) & ((side_row < SR + 1) | has_below)
+    for s, open_ in enumerate((c > 0, c < cols - 1)):
+        total = None
+        for a in range(3):
+            term = jnp.dot(side_in[s, a : a + SR + 2, :].astype(BF), w1_ref[a], preferred_element_type=F32)
+            total = term if total is None else total + term
+        side_first[s, 0 : SR + 2, :] = jnp.where(inside & open_, silu(total + b1_ref[...]), 0.0)
+    for i in range(SR + 2):
+        row = first[i].astype(F32)
+        if i == 0:
+            row = jnp.where(has_above, row, 0.0)
+        if i == SR + 1:
+            row = jnp.where(has_below, row, 0.0)
+        shifts(i, row)
+    for i in range(SR + 2):
+        wide[i, 0:1, 0:C] = side_first[0, i : i + 1, :].astype(BF)
+        wide[i, TC - 1 : TC, 2 * C :] = side_first[1, i : i + 1, :].astype(BF)
+    block_rows = PH // 2
 
     count = PATCHES // 2
     values = (values0, values1)
@@ -445,9 +494,9 @@
             gather_copy(q, across, way, way, 2, half_of(q, across, way)).wait_recv()
 
     for h in range(2):
-        halves = []
+        halves, others = [], []
         for i in range(h * PH, (h + 1) * PH, block_rows):
-            v = convolved(i, w2_ref, b2_ref).reshape(block_rows, TC, C)
+            v = convolved(i, block_rows, w2_ref, b2_ref).reshape(block_rows, TC, C)
             v = (tile[i : i + block_rows].astype(F32) + v).astype(BF)
             grid_ref[i : i + block_rows] = v
             halves.append(v)
@@ -455,13 +504,19 @@
             lower = halves[0][:, w * PW : (w + 1) * PW, :].reshape(FOLD, C)
             upper = halves[1][:, w * PW : (w + 1) * PW, :].reshape(FOLD, C)
             mine[0, h * count + w] = jnp.where(low_lanes, lower, swapped(upper).astype(BF))
-            mine[1, h * count + w] = jnp.where(low_lanes, swapped(lower).astype(BF), upper)
+            others.append((h * count + w, lower, upper))
         gather_start(0, h)
+        for at, lower, upper in others:
+            mine[1, at] = jnp.where(low_lanes, swapped(lower).astype(BF), upper)
+    grid_copy = pltpu.make_async_copy(grid_ref, grid_hbm, grid_sem)
+    grid_copy.start()
     for q in range(2):
         values[q][pl.ds(z * PATCHES, PATCHES)] = mine[q]
+    lax.fori_loop(2 * quarter, 3 * quarter, prepare, 0)
     gather_relay(0)
     gather_start(1, 0)
     gather_start(1, 1)
+    lax.fori_loop(3 * quarter, tiles, prepare, 0)
     gather_finish(0)
 
     def swap_values(q):
@@ -471,24 +526,13 @@
 
         lax.fori_loop(0, ORBITS * PATCHES, one, 0)
 
-    one_block = jnp.ones((BLK, C), BF)
-    one_low, one_high = jnp.where(low_lanes, one_block, zero_block), jnp.where(low_lanes, zero_block, one_block)
-
     def read(q, j, target_ref):
-        patches = [links_smem[2, j * MOST + i] for i in range(MOST)]
-        a, b = patches
-        low0 = jnp.where(low_lanes, values[q][a], zero_block)
-        low1 = jnp.where(low_lanes, values_swapped[q, a], zero_block)
-        high0 = jnp.where(low_lanes, zero_block, values_swapped[q, b])
-        high1 = jnp.where(low_lanes, zero_block, values[q][b])
+        a, b = [links_smem[2, j * MOST + i] for i in range(MOST)]
         right = jnp.concatenate([
-            jnp.concatenate([low0, one_low], axis=1), jnp.concatenate([low1, one_low], axis=1),
-            jnp.concatenate([high0, one_high], axis=1), jnp.concatenate([high1, one_high], axis=1),
+            jnp.where(low_lanes, values[q][a], zero_block), jnp.where(low_lanes, values_swapped[q, a], zero_block),
+            jnp.where(low_lanes, zero_block, values_swapped[q, b]), jnp.where(low_lanes, zero_block, values[q][b]),
         ], axis=0)
-        left = jnp.concatenate([matrices[j * MOST], matrices[j * MOST + 1]], axis=0)
-        summed = lax.dot_general(left, right, (((0,), (0,)), ((), ())), preferred_element_type=F32)
-        total = jnp.where(summed[:, C:] > 0.0, summed[:, C:], 1.0)
-        target_ref[j] = (summed[:, :C] / total).astype(BF)
+        target_ref[j] = (jnp.dot(turned[j], right, preferred_element_type=F32) * inverse[j]).astype(BF)
 
     back = (back0, back1)
 
@@ -499,22 +543,29 @@
         )
 
     def read_and_send(q):
-        def step(j, carry):
-            read(q, j, back_out.at[q])
-            back_copy(q, j).start()
+        def step(p, carry):
+            for u in range(2):
+                read(q, 2 * p + u, back_out.at[q])
+            for u in range(2):
+                back_copy(q, 2 * p + u).start()
             return carry
 
         return step
 
+    def read_first(q):
+        read(q, 1, back_out.at[q])
+        back_copy(q, 1).start()
+        read(q, 0, back[q])
+
     swap_values(0)
-    lax.fori_loop(1, tiles // 2, read_and_send(0), 0)
+    read_first(0)
+    lax.fori_loop(1, quarter, read_and_send(0), 0)
     gather_relay(1)
-    lax.fori_loop(tiles // 2, tiles, read_and_send(0), 0)
-    read(0, 0, back0)
+    lax.fori_loop(quarter, tiles // 2, read_and_send(0), 0)
     gather_finish(1)
     swap_values(1)
-    lax.fori_loop(1, tiles, read_and_send(1), 0)
-    read(1, 0, back1)
+    read_first(1)
+    lax.fori_loop(1, tiles // 2, read_and_send(1), 0)
 
     def arrive(q):
         def step(j, carry):
@@ -536,13 +587,23 @@
                 x = back[q][j].astype(F32)
                 value = (features[b].astype(F32) + jnp.where(in_place, x, swapped(x))).astype(BF)
                 out_ref[b] = value if q == 0 else jnp.where(low_lanes, out_ref[b], value)
+            if q == 1:
+                store(i).start()
             return carry
 
         return step
+
+    def store(i):
+        some = pl.ds(i * together, together)
+        return pltpu.make_async_copy(out_ref.at[some], out_hbm.at[some], store_sem.at[i])
 
     for q in range(2):
         lax.fori_loop(1, tiles, arrive(q), 0)
         lax.fori_loop(0, blocks // together, combine(q), 0)
+
+    def stored(i, carry):
+        store(i).wait()
+        return carry
 
     def sent(j, carry):
         for q in range(2):
@@ -551,6 +612,8 @@
         return carry
 
     lax.fori_loop(1, tiles, sent, 0)
+    lax.fori_loop(0, blocks // together, stored, 0)
+    grid_copy.wait()
     for q in range(2):
         for copies in rings[q]:
             for copy in copies:
@@ -578,8 +641,10 @@
         grid=(1,),
         out_shape=(jax.ShapeDtypeStruct((blocks, BLK, C), BF), jax.ShapeDtypeStruct((SR, TC, C), BF)),
         in_specs=[sm, vm, vm] + [pl.BlockSpec(memory_space=pl.ANY)] * 5 + [vm] * 7,
-        out_specs=(vm, vm),
+        out_specs=(pl.BlockSpec(memory_space=pl.ANY),) * 2,
         scratch_shapes=[
+            VMEM((blocks, BLK, C), BF),
+            VMEM((SR, TC, C), BF),
             VMEM((blocks, BLK, C), BF),
             VMEM((2, blocks * BLK), BF),
             VMEM((8, blocks * BLK), jnp.int32),
@@ -596,6 +661,8 @@
             VMEM((tiles, BLK, C), BF),
             VMEM((slots, CELLS, BLK), BF),
             VMEM((slots, 8, BLK), F32),
+            VMEM((tiles, BLK, MOST * CELLS), BF),
+            VMEM((tiles, BLK, C), F32),
             VMEM((slots + 1, FOLD, C), F32),
             VMEM((slots + 1, FOLD, C), F32),
             VMEM((slots + 1, 8, CELLS), F32),
@@ -610,11 +677,13 @@
             VMEM((2, 2, part_rows, C), BF),
             VMEM((PATCHES, FOLD, C), F32),
             VMEM((SR, TC, C), BF),
-            VMEM((SR + 2, TC, 3 * C), BF),
-            VMEM((SR, TC, C), BF),
+            VMEM((SR + 4, TC, 3 * C), BF),
+            VMEM((SR + 2, TC, C), BF),
+            VMEM((2, SR + 8, 3 * C), F32),
+            VMEM((2, SR + 8, C), F32),
             VMEM((2, 2, SR, C), BF),
             VMEM((2, 2, TC, C), BF),
-            VMEM((2, 6, SR, C), BF),
+            VMEM((6, 2, SR, C), BF),
             VMEM((2, PATCHES, FOLD, C), BF),
             VMEM((patches, FOLD, C), BF),
             VMEM((patches, FOLD, C), BF),
@@ -626,14 +695,16 @@
             dma((2, tiles)),
             dma((2, 2, 3)),
             dma((2, 2, 3)),
-            dma((2, 8)),
-            dma((2, 8)),
+            dma((8,)),
+            dma((8,)),
             dma((2, 2, 3)),
             dma((2, 2, 3)),
             dma((2, tiles)),
             dma((2, tiles)),
             dma((2,)),
             dma((6,)),
+            dma((blocks // min(4, blocks),)),
+            dma,
         ],
         compiler_params=pltpu.CompilerParams(collective_id=0, has_side_effects=True, vmem_limit_bytes=63000000),
         name="encode",

time: 111 us -> 106 us (0.955)
  Pallas kernels: 107 us -> 102 us
    pallas_call x1, Pallas kernels: 107 us -> 102 us  [local(): pl.pallas_call(functools.partial(main_kernel, rows, cols, blocks), grid=(...]
where the time goes in v5:
time: 106 us
  Pallas kernels  102 us (96%)
  local copies, waits for them, and re-layouts  3.12 us (3%)
    pallas_call x1, Pallas kernels, local(): pl.pallas_call(functools.partial(main_kernel, rows, cols, blocks), grid=(...  102 us
    unnamed x4, local copies, waits for them, and re-layouts  3.12 us

profile of v5, /device:TPU:2, one launch (start us, length us, event | category | flops | bytes accessed | tf_op | source)
XLA Modules:
  0.0 105.6 jit_solution(9538246697251651705)
XLA Ops:
  0.6 101.8 %encode.1 = (bf16[32,128,128]{2,1,0:T(8,128)(2,1)}, bf16[16,128,128]{2,1,0:T(8,128)(2,1)}) custom-call(s32[32]{0:T(128)} %tile_of.1, s32[1,32]{1,0:T(1,128)} %bitcast.15, s32[1,32]{1,0:T(1,128)} %bitcast.16, bf16[32,128,128]{2,1,0:T(8,128)(2,1)} %bitcast.12, bf16[2,4096]{1,0:T(2,128)(2,1)} %off_hbm.1, s32[16,4096]{1,0:T(8,128)} %cells_hbm.1, ...), custom_call_target="tpu_custom_call" | custom-call | tf_op jit(solution)/shard_map/encode/pallas_call | solution.py:639
  102.5 0.0 copy-start
  102.5 2.3 %copy.18 = bf16[4096,128]{1,0:T(8,128)(2,1)} copy(bf16[4096,128]{1,0:T(8,128)(2,1)} %bitcast.11) | data formatting | bytes 2097152
  104.8 0.0 copy-done
  104.8 0.8 copy.19
Async XLA Ops:
  102.5 2.3 %copy-start = (bf16[16,128,128]{2,1,0:T(8,128)(2,1)S(1)}, bf16[16,128,128]{2,1,0:T(8,128)(2,1)}, u32[]{:S(2)}) copy-start(bf16[16,128,128]{2,1,0:T(8,128)(2,1)} %get-tuple-element.9) | copy-start | bytes 1572868

commit v6 on v5

--- a/solution.py
+++ b/solution.py
@@ -121,7 +121,7 @@
     table_copy = pltpu.make_async_copy(table, table_smem, link_sem.at[1])
     table_copy.start()
 
-    group = min(4, half_blocks)
+    group = min(8, half_blocks)
     proj = jnp.concatenate([wp_ref[...], swapped(wp_ref[...]).astype(BF)], axis=1)
     proj_bias = jnp.concatenate([bp_ref[...], jnp.concatenate([bp_ref[:, HALF:], bp_ref[:, :HALF]], axis=1)], axis=1)
 
@@ -520,11 +520,12 @@
     gather_finish(0)
 
     def swap_values(q):
-        def one(p, carry):
-            values_swapped[q, p] = swapped(values[q][p]).astype(BF)
+        def some(i, carry):
+            for u in range(PATCHES):
+                values_swapped[q, i * PATCHES + u] = swapped(values[q][i * PATCHES + u]).astype(BF)
             return carry
 
-        lax.fori_loop(0, ORBITS * PATCHES, one, 0)
+        lax.fori_loop(0, ORBITS, some, 0)
 
     def read(q, j, target_ref):
         a, b = [links_smem[2, j * MOST + i] for i in range(MOST)]
@@ -620,6 +621,21 @@
                 copy.wait_send()
     for copy in gathers + edge_copies:
         copy.wait_send()
+
+
+def copy_kernel(pieces, out_main, grid_main, out_hbm, grid_hbm, out_v, grid_v, in_sem, to_sem):
+    rows = out_v.shape[0] // pieces
+    sets = [(out_main.at[pl.ds(i * rows, rows)], out_v.at[pl.ds(i * rows, rows)], out_hbm.at[pl.ds(i * rows, rows)]) for i in range(pieces)]
+    sets.append((grid_main, grid_v, grid_hbm))
+    ins = [pltpu.make_async_copy(a, b, in_sem.at[i]) for i, (a, b, _) in enumerate(sets)]
+    outs = [pltpu.make_async_copy(b, d, to_sem.at[i]) for i, (_, b, d) in enumerate(sets)]
+    for x in ins:
+        x.start()
+    for x, y in zip(ins, outs):
+        x.wait()
+        y.start()
+    for y in outs:
+        y.wait()
 
 
 def local(
@@ -713,6 +729,15 @@
         w_first.reshape(3, 3 * C, C), w_second.reshape(3, 3 * C, C), w_embed, b_embed[None, :], w_proj, b_proj[None, :],
         density_weight[None, :], b_first[None, :], b_second[None, :],
     )
+    pieces = 4
+    obs_out, grid_out = pl.pallas_call(
+        functools.partial(copy_kernel, pieces),
+        out_shape=(jax.ShapeDtypeStruct((blocks, BLK, C), BF), jax.ShapeDtypeStruct((SR, TC, C), BF)),
+        in_specs=[pl.BlockSpec(memory_space=pl.ANY)] * 2,
+        out_specs=(pl.BlockSpec(memory_space=pl.ANY),) * 2,
+        scratch_shapes=[VMEM((blocks, BLK, C), BF), VMEM((SR, TC, C), BF), dma((pieces + 1,)), dma((pieces + 1,))],
+        name="copy_out",
+    )(obs_out, grid_out)
     return (obs_out.reshape(obs_feat.shape), grid_out)
 
 

time: 106 us -> 104 us (0.981)
  local copies, waits for them, and re-layouts: 3.12 us -> 0 us
    unnamed x4 -> x0, local copies, waits for them, and re-layouts: 3.12 us -> none
    pallas_call x0 -> x1, Pallas kernels: none -> 2.24 us  [local(): pl.pallas_call(functools.partial(copy_kernel, pieces), out_shape=(jax.Sha...]
    pallas_call x1, Pallas kernels: 102 us -> 100 us  [local(): pl.pallas_call(functools.partial(main_kernel, rows, cols, blocks), grid=(...]
where the time goes in v6:
time: 104 us; the launch traced here: 103 us
  Pallas kernels  103 us (99%)
    pallas_call x1, Pallas kernels, local(): pl.pallas_call(functools.partial(main_kernel, rows, cols, blocks), grid=(...  100 us
    pallas_call x1, Pallas kernels, local(): pl.pallas_call(functools.partial(copy_kernel, pieces), out_shape=(jax.Sha...  2.24 us

profile of v6, /device:TPU:2, one launch (start us, length us, event | category | flops | bytes accessed | tf_op | source)
XLA Modules:
  0.0 103.3 jit_solution(12540010874125426656)
XLA Ops:
  0.6 100.4 %encode.1 = (bf16[32,128,128]{2,1,0:T(8,128)(2,1)}, bf16[16,128,128]{2,1,0:T(8,128)(2,1)}) custom-call(s32[32]{0:T(128)} %tile_of.1, s32[1,32]{1,0:T(1,128)} %bitcast.14, s32[1,32]{1,0:T(1,128)} %bitcast.15, bf16[32,128,128]{2,1,0:T(8,128)(2,1)} %bitcast.11, bf16[2,4096]{1,0:T(2,128)(2,1)} %off_hbm.1, s32[16,4096]{1,0:T(8,128)} %cells_hbm.1, ...), custom_call_target="tpu_custom_call" | custom-call | tf_op jit(solution)/shard_map/encode/pallas_call | solution.py:655
  101.1 2.2 %copy_out.1 = (bf16[32,128,128]{2,1,0:T(8,128)(2,1)}, bf16[16,128,128]{2,1,0:T(8,128)(2,1)}) custom-call(bf16[32,128,128]{2,1,0:T(8,128)(2,1)} %get-tuple-element.6.out_main, bf16[16,128,128]{2,1,0:T(8,128)(2,1)} %get-tuple-element.7.grid_main), custom_call_target="tpu_custom_call" | custom-call | tf_op jit(solution)/shard_map/copy_out/pallas_call | solution.py:733

commit v7 on v6

--- a/solution.py
+++ b/solution.py
@@ -82,18 +82,6 @@
         return (other // rows, other % rows, (c + cols + side) % cols)
 
     edges = ((-1, 0), (1, 0), (-1, -1), (0, -1), (1, -1), (-1, 1), (0, 1), (1, 1))
-    barrier = pltpu.get_barrier_semaphore()
-
-    def greet(j, carry):
-        pl.semaphore_signal(barrier, inc=1, device_id=(z, *target(j)), device_id_type=MESH)
-        return carry
-
-    lax.fori_loop(1, tiles, greet, 0)
-    for other in (after, before):
-        pl.semaphore_signal(barrier, inc=1, device_id=(other, r, c), device_id_type=MESH)
-    for up, side in edges:
-        pl.semaphore_signal(barrier, inc=1, device_id=edge_device(up, side), device_id_type=MESH)
-
     half_blocks = blocks // 2
     loads = [
         pltpu.make_async_copy(feat_hbm.at[pl.ds(0, half_blocks)], feat_ref.at[pl.ds(0, half_blocks)], load_sem.at[0]),
@@ -105,6 +93,18 @@
     ]
     for load in loads:
         load.start()
+
+    barrier = pltpu.get_barrier_semaphore()
+
+    def greet(j, carry):
+        pl.semaphore_signal(barrier, inc=1, device_id=(z, *target(j)), device_id_type=MESH)
+        return carry
+
+    lax.fori_loop(1, tiles, greet, 0)
+    for other in (after, before):
+        pl.semaphore_signal(barrier, inc=1, device_id=(other, r, c), device_id_type=MESH)
+    for up, side in edges:
+        pl.semaphore_signal(barrier, inc=1, device_id=edge_device(up, side), device_id_type=MESH)
 
     square = (tiles, blocks)
     block_id = lax.broadcasted_iota(jnp.int32, square, 1).astype(F32)
@@ -315,7 +315,7 @@
     receive1(0)
     out_copy(1, 1).wait_recv()
     receive1(1)
-    middle = max(1, tiles // 4)
+    middle = max(1, 3 * tiles // 8)
     lax.fori_loop(1, middle, step1, 0)
     ring_relay(0)
     lax.fori_loop(middle, tiles // 2, step1, 0)

time: 104 us -> 103 us (level)
  Pallas kernels: 103 us -> 101 us
    pallas_call x1, Pallas kernels: 100 us -> 98.7 us  [local(): pl.pallas_call(functools.partial(main_kernel, rows, cols, blocks), grid=(...]
where the time goes in v7:
time: 103 us; the launch traced here: 102 us
  Pallas kernels  101 us (98%)
    pallas_call x1, Pallas kernels, local(): pl.pallas_call(functools.partial(main_kernel, rows, cols, blocks), grid=(...  98.7 us
    pallas_call x1, Pallas kernels, local(): pl.pallas_call(functools.partial(copy_kernel, pieces), out_shape=(jax.Sha...  2.24 us

profile of v7, /device:TPU:2, one launch (start us, length us, event | category | flops | bytes accessed | tf_op | source)
XLA Modules:
  0.0 101.6 jit_solution(2144459847540795499)
XLA Ops:
  0.6 98.7 %encode.1 = (bf16[32,128,128]{2,1,0:T(8,128)(2,1)}, bf16[16,128,128]{2,1,0:T(8,128)(2,1)}) custom-call(s32[32]{0:T(128)} %tile_of.1, s32[1,32]{1,0:T(1,128)} %bitcast.14, s32[1,32]{1,0:T(1,128)} %bitcast.15, bf16[32,128,128]{2,1,0:T(8,128)(2,1)} %bitcast.11, bf16[2,4096]{1,0:T(2,128)(2,1)} %off_hbm.1, s32[16,4096]{1,0:T(8,128)} %cells_hbm.1, ...), custom_call_target="tpu_custom_call" | custom-call | tf_op jit(solution)/shard_map/encode/pallas_call | solution.py:655
  99.4 2.2 %copy_out.1 = (bf16[32,128,128]{2,1,0:T(8,128)(2,1)}, bf16[16,128,128]{2,1,0:T(8,128)(2,1)}) custom-call(bf16[32,128,128]{2,1,0:T(8,128)(2,1)} %get-tuple-element.6.out_main, bf16[16,128,128]{2,1,0:T(8,128)(2,1)} %get-tuple-element.7.grid_main), custom_call_target="tpu_custom_call" | custom-call | tf_op jit(solution)/shard_map/copy_out/pallas_call | solution.py:733
